TPU v7x, 256 devices: a whole 4x4x8 slice. The times are simulated.
256 devices in a mesh: rep: 4 (over y_lo, core), dp: 64 (over z, x, y_hi).
Axes of the slice: x: 4, y: 4 (y_hi: 2, y_lo: 2; y = y_hi * 2 + y_lo), z: 8, core: 2. Of those that a mesh axis runs over, the one named last changes fastest.
Arguments:
- first_core: float32 [512, 512], P('dp'), may hold values from -6 to 6
- first_moment: float32 [512, 512], P('dp'), may hold values from -4 to 4
- first_second: float32 [512, 512], P('dp'), may hold values from 0.01 to 1
- mid_core: float32 [256, 131072], P('dp'), may hold values from -0.5 to 0.5
- mid_moment: float32 [256, 131072], P('dp'), may hold values from -4 to 4
- mid_second: float32 [256, 131072], P('dp'), may hold values from 0.01 to 1
- last_core: float32 [512, 512], P('dp'), may hold values from -0.5 to 0.5
- last_moment: float32 [512, 512], P('dp'), may hold values from -4 to 4
- last_second: float32 [512, 512], P('dp'), may hold values from 0.01 to 1
- cotangent: bfloat16 [4096, 128], P(('rep', 'dp')), may hold values from -6 to 6
- bag_lengths: int32 [256, 16], P(('rep', 'dp')), may hold values from 1 to 32, 256 in all within a row
- first_digit: int32 [65536], P(('rep', 'dp')), may hold values from 0 to 511
- mid_digit: int32 [65536, 1], P(('rep', 'dp')), may hold values from 0 to 255; in each aligned block of 256 rows (0 to 255, 256 to 511, ...) at most 2 rows name the same one
- last_digit: int32 [65536], P(('rep', 'dp')), may hold values from 0 to 511
Outputs:
- first_core_next: float32 [512, 512], P('dp')
- first_moment_next: float32 [512, 512], P('dp')
- first_second_next: float32 [512, 512], P('dp')
- mid_core_next: float32 [256, 131072], P('dp')
- mid_moment_next: float32 [256, 131072], P('dp')
- mid_second_next: float32 [256, 131072], P('dp')
- last_core_next: float32 [512, 512], P('dp')
- last_moment_next: float32 [512, 512], P('dp')
- last_second_next: float32 [512, 512], P('dp')
Inputs may be any that keep to these rules, and one draw needn't show every extreme that they name: `mid_digit`: within each block of 256 lookups no middle digit appears more than 2 times, and in some block one digit appears exactly 2 times. `bag_lengths`: each row sums to 256; some entry of each row equals 32.
All inputs are finite; a program needn't handle non-finite values.
Results may differ from a plain program's by a relative error of at most 0.0056.
Values may be sent and summed in bfloat16 or wider, within the bound.
No kernel may reach another device: no remote copies, remote signals or barrier semaphores. Data moves between devices by JAX's collectives and lax.ppermute only.
A program may use at most 64 MiB of HBM per device.

v0:
```python
from functools import partial

import jax
import jax.numpy as jnp
from jax import lax
from jax.sharding import PartitionSpec as P

N2 = 256
N3 = 512
R = 128
D1 = 4
D2 = 8
D3 = 4
STEP = 20
CAP = 2


LEARN_RATE = 0.01
BETA_ONE = 0.9
BETA_TWO = 0.999
EPSILON = 1e-08


def adam_update(current, moment, second, gradient):
    moment_next = BETA_ONE * moment + (1.0 - BETA_ONE) * gradient
    second_next = BETA_TWO * second + (1.0 - BETA_TWO) * gradient * gradient
    corrected = moment_next / (1.0 - BETA_ONE**STEP)
    spread = jnp.sqrt(second_next / (1.0 - BETA_TWO**STEP))
    return (current - LEARN_RATE * corrected / (spread + EPSILON), moment_next, second_next)


def slot_terms(row_items, first_copy, last_copy):
    slot_grads, slot_pairs, mid_row = row_items
    slot_count = slot_grads.shape[0]
    tail_rows = last_copy.shape[0]
    grad_cube = slot_grads.reshape(slot_count, D1, D2, D3)
    first_rows = first_copy[slot_pairs // tail_rows].reshape(slot_count, D1, R)
    last_rows = last_copy[slot_pairs % tail_rows].reshape(slot_count, R, D3)
    mid_cube = mid_row.reshape(R, D2, R)
    first_mix = jnp.einsum(
        "kar,kabc->krbc", first_rows, grad_cube, preferred_element_type=jnp.float32
    ).astype(jnp.bfloat16)
    mid_term = jnp.einsum("krbc,ksc->rbs", first_mix, last_rows, preferred_element_type=jnp.float32)
    tail_mix = jnp.einsum(
        "rbs,ksc->krbc", mid_cube, last_rows, preferred_element_type=jnp.float32
    ).astype(jnp.bfloat16)
    first_term = jnp.einsum(
        "kabc,krbc->kar", grad_cube, tail_mix, preferred_element_type=jnp.float32
    )
    head_mix = jnp.einsum(
        "kar,rbs->kabs", first_rows, mid_cube, preferred_element_type=jnp.float32
    ).astype(jnp.bfloat16)
    last_term = jnp.einsum(
        "kabs,kabc->ksc", head_mix, grad_cube, preferred_element_type=jnp.float32
    )
    return (
        mid_term.reshape(-1),
        first_term.reshape(slot_count, D1 * R),
        last_term.reshape(slot_count, R * D3),
    )


def core_terms(slot_grads, slot_pairs, mid_copy, first_copy, last_copy):
    per_row = lax.map(
        partial(slot_terms, first_copy=first_copy, last_copy=last_copy),
        (slot_grads, slot_pairs, mid_copy),
    )
    mid_part, first_terms, last_terms = per_row
    tail_rows = last_copy.shape[0]
    flat_pairs = slot_pairs.reshape(-1)
    first_part = jax.ops.segment_sum(
        first_terms.reshape(-1, first_terms.shape[-1]),
        flat_pairs // tail_rows,
        num_segments=first_copy.shape[0],
    )
    last_part = jax.ops.segment_sum(
        last_terms.reshape(-1, last_terms.shape[-1]), flat_pairs % tail_rows, num_segments=tail_rows
    )
    return (mid_part, first_part, last_part)


def local(
    first_core,
    first_moment,
    first_second,
    mid_core,
    mid_moment,
    mid_second,
    last_core,
    last_moment,
    last_second,
    cotangent,
    bag_lengths,
    first_digit,
    mid_digit,
    last_digit,
):
    dp_count = lax.axis_size("dp")
    local_rows = mid_core.shape[0]
    look_count = first_digit.shape[0]
    embed_dim = cotangent.shape[1]
    positions = jnp.arange(look_count, dtype=jnp.int32)
    bag_ends = jnp.cumsum(bag_lengths[0])
    sample_of = jnp.sum((bag_ends[None, :] <= positions[:, None]).astype(jnp.int32), axis=1)
    mid_rows = mid_digit[:, 0]
    earlier = (mid_rows[None, :] == mid_rows[:, None]) & (positions[None, :] < positions[:, None])
    slot_index = mid_rows * CAP + jnp.sum(earlier.astype(jnp.int32), axis=1)
    payload = (
        jnp.zeros((N2 * CAP, embed_dim), jnp.bfloat16).at[slot_index].set(cotangent[sample_of])
    )
    pair_ids = jnp.zeros((N2 * CAP,), jnp.int32).at[slot_index].set(first_digit * N3 + last_digit)
    first_copy, last_copy = (
        lax.all_gather(first_core.astype(jnp.bfloat16), "dp", axis=0, tiled=True),
        lax.all_gather(last_core.astype(jnp.bfloat16), "dp", axis=0, tiled=True),
    )
    mid_copy = mid_core.astype(jnp.bfloat16)
    payload = payload.reshape(dp_count, local_rows, CAP, embed_dim)
    pair_ids = pair_ids.reshape(dp_count, local_rows, CAP)
    arrived, arrived_ids = (
        lax.all_to_all(payload, "dp", split_axis=0, concat_axis=2, tiled=True),
        lax.all_to_all(pair_ids, "dp", split_axis=0, concat_axis=2, tiled=True),
    )
    mid_grad, first_part, last_part = core_terms(
        arrived[0], arrived_ids[0], mid_copy, first_copy, last_copy
    )
    mid_grad = lax.psum(mid_grad, "rep")
    shares = (
        lax.psum_scatter(first_part, "dp", scatter_dimension=0, tiled=True),
        lax.psum_scatter(last_part, "dp", scatter_dimension=0, tiled=True),
    )
    first_grad, last_grad = lax.psum((shares[0], shares[1]), "rep")
    first_next = adam_update(first_core, first_moment, first_second, first_grad)
    mid_next = adam_update(mid_core, mid_moment, mid_second, mid_grad)
    last_next = adam_update(last_core, last_moment, last_second, last_grad)
    return (
        first_next[0],
        first_next[1],
        first_next[2],
        mid_next[0],
        mid_next[1],
        mid_next[2],
        last_next[0],
        last_next[1],
        last_next[2],
    )


def solution(mesh):
    return jax.shard_map(
        local,
        mesh=mesh,
        in_specs=(
            P("dp", None),
            P("dp", None),
            P("dp", None),
            P("dp", None),
            P("dp", None),
            P("dp", None),
            P("dp", None),
            P("dp", None),
            P("dp", None),
            P(("rep", "dp"), None),
            P(("rep", "dp"), None),
            P(("rep", "dp")),
            P(("rep", "dp"), None),
            P(("rep", "dp")),
        ),
        out_specs=(
            P("dp", None),
            P("dp", None),
            P("dp", None),
            P("dp", None),
            P("dp", None),
            P("dp", None),
            P("dp", None),
            P("dp", None),
            P("dp", None),
        ),
        check_vma=False,
    )
```

profile of v0, /device:TPU:1, one launch (start us, length us, event | category | flops | bytes accessed | tf_op | source)
XLA Modules:
  0.0 1317.2 jit_solution(478008446788898712)
XLA Ops:
  13.1 15.1 %all-to-all-start = ((s32[64,4,2]{1,2,0:T(2,128)}), s32[64,4,2]{1,2,0:T(2,128)S(1)}, u32[]{:S(2)}, u32[]{:S(2)}) async-start(s32[64,4,2]{1,2,0:T(2,128)} %copy.92), calls=%async_computation | async-start | bytes 131072 | tf_op jit(solution)/shard_map/all_to_all | solution.py:121
  30.6 156.3 %all_gather.7 = bf16[512,512]{1,0:T(8,128)(2,1)S(1)} all-gather(bf16[8,512]{1,0:T(8,128)(2,1)S(1)} %convert_element_type.39), channel_id=1, replica_groups=mesh['rep'=4,'dp'=64] {'dp'}, dimensions={0}, use_global_device_ids=true | all-gather | bytes 532480 | tf_op jit(solution)/shard_map/all_gather | solution.py:114
  186.9 149.4 %all_gather.6 = bf16[512,512]{1,0:T(8,128)(2,1)S(1)} all-gather(bf16[8,512]{1,0:T(8,128)(2,1)S(1)} %convert_element_type.37), channel_id=1, replica_groups=mesh['rep'=4,'dp'=64] {'dp'}, dimensions={0}, use_global_device_ids=true | all-gather | bytes 532480 | tf_op jit(solution)/shard_map/all_gather | solution.py:113
  336.3 2.9 convert_element_type.40
  341.7 7.3 all-to-all-start.1
  350.0 10.2 all-to-all-done.1
  360.3 135.0 %while.16 = (s32[]{:T(128)}, f32[4,131072]{1,0:T(4,128)}, f32[4,128,512]{2,1,0:T(8,128)}, f32[4,128,512]{2,1,0:T(8,128)}, s32[4,128]{1,0:T(4,128)S(1)}, /*index=...) while((s32[]{:T(128)}, f32[4,131072]{1,0:T(4,128)}, ...), condition=%wide.region_6.7_spmd, body=%wide.region_5.6_spmd.sunk | while | flops 416814720 | bytes 20165912 | solution.py:64
  364.3 2.8 dynamic-slice_reduce_fusion.2
  377.9 2.9 copy.151
  382.8 10.5 dynamic_update_slice.25
  398.0 2.8 dynamic-slice_reduce_fusion.2
  411.6 2.9 copy.151
  416.5 10.5 dynamic_update_slice.25
  431.8 2.8 dynamic-slice_reduce_fusion.2
  445.3 2.9 copy.151
  450.2 10.5 dynamic_update_slice.25
  479.1 2.9 copy.151
  484.0 10.5 dynamic_update_slice.25
  495.3 5.2 scatter_custom_fusion.2
  500.9 5.4 scatter_custom_fusion.3
  506.9 366.9 %reduce-scatter.3.cloned.1.call-done = f32[8,512]{1,0:T(8,128)} async-done(((f32[512,512]{1,0:T(8,128)}), f32[8,512]{1,0:T(8,128)}) %reduce-scatter.3.cloned.1.call-update) | async-done | bytes 16400 | tf_op jit(solution)/shard_map/reduce_scatter | solution.py:128
  873.8 366.4 %reduce-scatter.5.cloned.1.call-done = f32[8,512]{1,0:T(8,128)} async-done(((f32[512,512]{1,0:T(8,128)}), f32[8,512]{1,0:T(8,128)}) %reduce-scatter.5.cloned.1.call-update) | async-done | bytes 16400 | tf_op jit(solution)/shard_map/reduce_scatter | solution.py:129
  1240.2 62.4 %all-reduce = (f32[8,512]{1,0:T(8,128)S(1)}, f32[8,512]{1,0:T(8,128)S(1)}) all-reduce(f32[8,512]{1,0:T(8,128)} %reduce-scatter.3.cloned.1.call-done, f32[8,512]{1,0:T(8,128)} %reduce-scatter.5.cloned.1.call-done), channel_id=1, replica_groups=mesh['rep'=4,'dp'=64] {'rep'}, use_global_device_ids=true, to_apply=%region_9.10 | all-reduce | flops 8192 | bytes 65536 | tf_op jit(solution)/shard_map/psum | solution.py:131
  1303.3 6.5 divide_subtract_fusion
  (190 shorter events, 84.8 us)
Async XLA Ops:
  8.0 331.2 %copy-start = (bf16[16,128]{1,0:T(8,128)(2,1)S(1)}, bf16[16,128]{1,0:T(8,128)(2,1)}, u32[]{:S(2)}) copy-start(bf16[16,128]{1,0:T(8,128)(2,1)} %param.25) | copy-start | bytes 12292
  13.1 328.6 %all-to-all-start = ((s32[64,4,2]{1,2,0:T(2,128)}), s32[64,4,2]{1,2,0:T(2,128)S(1)}, u32[]{:S(2)}, u32[]{:S(2)}) async-start(s32[64,4,2]{1,2,0:T(2,128)} %copy.92), calls=%async_computation | async-start | bytes 131072 | tf_op jit(solution)/shard_map/all_to_all | solution.py:121
  341.7 18.6 %all-to-all-start.1 = ((bf16[64,4,2,128]{3,2,1,0:T(2,128)(2,1)}), bf16[64,4,2,128]{3,2,1,0:T(2,128)(2,1)S(1)}, u32[]{:S(2)}, u32[]{:S(2)}) async-start(bf16[64,4,2,128]{3,2,1,0:T(2,128)(2,1)} %bitcast.29), calls=%async_computation.1 | async-start | bytes 262144 | tf_op jit(solution)/shard_map/all_to_all | solution.py:120
  348.9 524.9 %reduce-scatter.3.cloned.1.call-start = ((), (), s32[]{:S(2)}) async-start(), calls=%async_computation.4 | async-start | bytes 1064960 | tf_op jit(solution)/shard_map/reduce_scatter | solution.py:128
  370.9 2.7 copy-start.3
  376.4 4.3 copy-start.2
  382.6 11.5 copy-start.6
  404.6 2.7 copy-start.3
  410.2 4.3 copy-start.2
  416.4 11.5 copy-start.6
  443.9 4.3 copy-start.2
  450.1 11.5 copy-start.6
  472.1 2.7 copy-start.3
  477.6 4.3 copy-start.2
  483.8 11.5 copy-start.6
  500.6 739.7 %reduce-scatter.5.cloned.1.call-start = ((), (), s32[]{:S(2)}) async-start(), calls=%async_computation.6 | async-start | bytes 1064960 | tf_op jit(solution)/shard_map/reduce_scatter | solution.py:129
  500.8 801.8 %copy-start.7 = (f32[8,512]{1,0:T(8,128)S(1)}, f32[8,512]{1,0:T(8,128)}, u32[]{:S(2)}) copy-start(f32[8,512]{1,0:T(8,128)} %param.22) | copy-start | bytes 49156
  500.8 801.7 %copy-start.8 = (f32[8,512]{1,0:T(8,128)S(1)}, f32[8,512]{1,0:T(8,128)}, u32[]{:S(2)}) copy-start(f32[8,512]{1,0:T(8,128)} %param.16) | copy-start | bytes 49156
  500.9 801.7 %copy-start.9 = (f32[8,512]{1,0:T(8,128)S(1)}, f32[8,512]{1,0:T(8,128)}, u32[]{:S(2)}) copy-start(f32[8,512]{1,0:T(8,128)} %param.23) | copy-start | bytes 49156
  500.9 801.7 %copy-start.10 = (f32[8,512]{1,0:T(8,128)S(1)}, f32[8,512]{1,0:T(8,128)}, u32[]{:S(2)}) copy-start(f32[8,512]{1,0:T(8,128)} %param.24) | copy-start | bytes 49156
  500.9 801.7 %copy-start.11 = (f32[8,512]{1,0:T(8,128)S(1)}, f32[8,512]{1,0:T(8,128)}, u32[]{:S(2)}) copy-start(f32[8,512]{1,0:T(8,128)} %param.18) | copy-start | bytes 49156
  500.9 801.7 %copy-start.12 = (f32[8,512]{1,0:T(8,128)S(1)}, f32[8,512]{1,0:T(8,128)}, u32[]{:S(2)}) copy-start(f32[8,512]{1,0:T(8,128)} %param.17) | copy-start | bytes 49156
  500.9 802.4 %copy-start.4 = (f32[4,131072]{1,0:T(4,128)S(1)}, f32[4,131072]{1,0:T(4,128)}, u32[]{:S(2)}) copy-start(f32[4,131072]{1,0:T(4,128)} %param.19) | copy-start | bytes 6291460
  506.3 797.0 %all-reduce.3.cloned.1.call-start = ((), (), s32[]{:S(2)}) async-start(), calls=%async_computation.5 | async-start | bytes 4194304 | tf_op jit(solution)/shard_map/psum | solution.py:126
  (9 other events, 10.2 us)
Sparse Core Ops, SparseCore 0:
  500.7 373.0 reduce-scatter.2
  876.8 363.3 reduce-scatter.4
Sparse Core Ops, SparseCore 1:
  510.0 115.3 all-reduce.2
where the time goes:
time: 1320 us
  waiting for transfers between devices  744 us (56%)
  blocking collectives  368 us (28%)
  local copies, waits for them, and re-layouts  108 us (8%)
  matrix products  32.4 us (2%)
  other arithmetic  25 us (2%)
  starting transfers between devices  22.9 us (2%)
  between operations  15.7 us (1%)
    reduce_scatter x1, waiting for transfers between devices, local(): lax.psum_scatter(first_part, 'dp', scatter_dimension=0, tiled=True)  367 us
    reduce_scatter x1, waiting for transfers between devices, local(): lax.psum_scatter(last_part, 'dp', scatter_dimension=0, tiled=True)  366 us
    all_gather x1, blocking collectives, local(): lax.all_gather(last_core.astype(jnp.bfloat16), 'dp', axis=0, tiled=True)  156 us
    all_gather x1, blocking collectives, local(): lax.all_gather(first_core.astype(jnp.bfloat16), 'dp', axis=0, tiled=True)  149 us
    psum x1, blocking collectives, local(): first_grad, last_grad = lax.psum((shares[0], shares[1]), 'rep')  62.4 us
    dynamic_update_slice x12, local copies, waits for them, and re-layouts, core_terms(): lax.map(partial(slot_terms, first_copy=first_copy, last_copy=last_copy),...  45.8 us
  transfers between devices with their start and end apart: 5, of which 3 were waited for; matrix products, arithmetic and copies ran while one was open for 1% of the time, Pallas kernels for 0%

commit v1 on v0

v1 whole, which is shorter than its diff:
```python
from functools import partial

import jax
import jax.numpy as jnp
from jax import lax
from jax.experimental import pallas as pl
from jax.experimental.pallas import tpu as pltpu
from jax.sharding import PartitionSpec as P

N2 = 256
R = 128
D1 = 4
D2 = 8
D3 = 4
STEP = 20
CAP = 2
LANES = 128
N_SRC = 64
SLOTS = 512
PER_ROW = 128
CHUNK = 16

LEARN_RATE = 0.01
BETA_ONE = 0.9
BETA_TWO = 0.999
EPSILON = 1e-08

BF = jnp.bfloat16
F32 = jnp.float32
INTERPRET = False


def adam_update(current, moment, second, gradient):
    moment_next = BETA_ONE * moment + (1.0 - BETA_ONE) * gradient
    second_next = BETA_TWO * second + (1.0 - BETA_TWO) * gradient * gradient
    corrected = moment_next / (1.0 - BETA_ONE**STEP)
    spread = jnp.sqrt(second_next / (1.0 - BETA_TWO**STEP))
    return (current - LEARN_RATE * corrected / (spread + EPSILON), moment_next, second_next)


def iota(shape, axis):
    return lax.broadcasted_iota(jnp.int32, shape, axis)


def nn(a, b):
    return lax.dot_general(a, b, (((1,), (0,)), ((), ())), preferred_element_type=F32)


def nt(a, b):
    return lax.dot_general(a, b, (((1,), (1,)), ((), ())), preferred_element_type=F32)


def tn(a, b):
    return lax.dot_general(a, b, (((0,), (0,)), ((), ())), preferred_element_type=F32)


def ones_where(cond):
    return jnp.where(cond, 1.0, 0.0).astype(BF)


def split_two(x):
    hi = x.astype(BF)
    return hi, (x - hi.astype(F32)).astype(BF)


def pack_kernel(side_ref, mid_ref, first_ref, last_ref, bag_ref, cot_ref, fcore_ref, lcore_ref, out_ref):
    count = mid_ref.shape[1]
    mids = jnp.broadcast_to(mid_ref[...].astype(F32), (count, count))
    row, col = iota((count, count), 0), iota((count, count), 1)
    mid_column = jnp.sum(jnp.where(row == col, mids, 0.0), axis=1, keepdims=True)
    earlier = (mid_column == mids) & (row < col)
    rank = jnp.sum(jnp.where(earlier, 1.0, 0.0), axis=0, keepdims=True)
    slot = mid_ref[...] * CAP + rank.astype(jnp.int32)
    place = ones_where(iota((SLOTS, count), 0) == slot)

    samples = bag_ref.shape[1]
    lens = jnp.broadcast_to(bag_ref[...].astype(F32), (samples, samples))
    n_row, n_col = iota((samples, samples), 0), iota((samples, samples), 1)
    ends = jnp.sum(jnp.where(n_col <= n_row, lens, 0.0), axis=1, keepdims=True)
    starts = jnp.sum(jnp.where(n_col < n_row, lens, 0.0), axis=1, keepdims=True)
    position = iota((samples, count), 1).astype(F32)
    owner = ones_where((position >= starts) & (position < ends))
    slot_owner = nt(place, owner).astype(BF)
    out_ref[:, 0:LANES] = nn(slot_owner, cot_ref[...]).astype(BF)

    field = iota((LANES, count), 0)
    first, last = first_ref[...], last_ref[...]
    fields = jnp.where(field == 0, first // 32, 0)
    fields = jnp.where(field == 1, first % 32, fields)
    fields = jnp.where(field == 2, last // 32, fields)
    fields = jnp.where(field == 3, last % 32, fields)
    out_ref[:, LANES : 2 * LANES] = nt(place, fields.astype(F32).astype(BF)).astype(BF)

    side = side_ref[0]
    width = fcore_ref.shape[1]
    core = jnp.where(side == 0, fcore_ref[...], lcore_ref[...])
    core = jnp.concatenate([core, core], axis=0).astype(BF)
    dest = iota((width, width), 1)
    source = jnp.where(side == 0, dest, (dest % LANES) * D3 + dest // LANES)
    core = nn(core, ones_where(iota((width, width), 0) == source)).astype(BF)
    for p in range(SLOTS // 16):
        out_ref[p * 16 : p * 16 + 16, 2 * LANES : 2 * LANES + width] = core


def pack(side, mid_digit, first_digit, last_digit, bag, cot, first_core, last_core):
    vmem = pl.BlockSpec(memory_space=pltpu.VMEM)
    return pl.pallas_call(
        pack_kernel,
        out_shape=jax.ShapeDtypeStruct((SLOTS, 2 * LANES + first_core.shape[1]), BF),
        in_specs=[pl.BlockSpec(memory_space=pltpu.SMEM)] + [vmem] * 7,
        out_specs=vmem,
        interpret=INTERPRET,
        name="pack",
    )(side, mid_digit, first_digit, last_digit, bag, cot, first_core, last_core)


def terms_kernel(
    side_ref, mine_ref, theirs_ref, mid_ref,
    midgrad_ref, keep_ref, send_ref,
    cores, arows, lrows, grads, head, mix_hi, mix_lo, fterm, lterm, midm, asub, midf,
):
    side = side_ref[0]
    width = cores.shape[2]
    cores[side] = mine_ref[:, 2 * LANES :]
    cores[1 - side] = theirs_ref[:, 2 * LANES :]
    new = iota((SLOTS, SLOTS), 0)
    old = (new % 64) * 8 + (new // 128) * 2 + (new // 64) % 2
    lane = iota((SLOTS, SLOTS), 1)
    slots = nn(ones_where(lane == old), mine_ref[:, 0 : 2 * LANES])
    grads[...] = slots[:, 0:LANES]
    first = slots[:, LANES : LANES + 1] * 32.0 + slots[:, LANES + 1 : LANES + 2]
    last = slots[:, LANES + 2 : LANES + 3] * 32.0 + slots[:, LANES + 3 : LANES + 4]
    lane_f = lane.astype(F32)
    pick_first = ones_where(lane_f == first)
    pick_last = ones_where(lane_f == last)
    arows[...] = nn(pick_first, cores[0]).astype(BF)
    lrows[...] = nn(pick_last, cores[1])

    def load_row(m):
        for b in range(D2):
            midm[:, b * LANES : (b + 1) * LANES] = mid_ref[
                pl.ds(b * 4 + m, R, stride=4 * D2), :
            ].astype(BF)
        for a in range(D1):
            asub[a * PER_ROW : (a + 1) * PER_ROW, :] = arows[
                m * PER_ROW : (m + 1) * PER_ROW, a * R : (a + 1) * R
            ]

    for m in range(4):
        load_row(m)
        head[m * SLOTS : (m + 1) * SLOTS, :] = nn(asub[...], midm[...]).astype(BF)

    def step(t, carry):
        n0 = pl.multiple_of(t * CHUNK, CHUNK)
        m = t // (PER_ROW // CHUNK)
        k0 = n0 - m * PER_ROW
        g = grads[pl.ds(n0, CHUNK), :]
        rows = [lrows[pl.ds(n0, CHUNK), c * LANES : (c + 1) * LANES] for c in range(D3)]
        sums = [jnp.zeros((CHUNK, LANES), F32) for _ in range(D3)]
        for a in range(D1):
            base = pl.multiple_of(m * SLOTS + a * PER_ROW + k0, CHUNK)
            for b in range(D2):
                at = a * D2 * D3 + b * D3
                h = head[pl.ds(base, CHUNK), b * LANES : (b + 1) * LANES].astype(F32)
                mix = None
                for c in range(D3):
                    spread = jnp.broadcast_to(g[:, at + c : at + c + 1], (CHUNK, LANES))
                    part = spread * rows[c]
                    mix = part if mix is None else mix + part
                    sums[c] = sums[c] + spread * h
                hi, lo = split_two(mix)
                mix_hi[pl.ds(base, CHUNK), b * LANES : (b + 1) * LANES] = hi
                mix_lo[pl.ds(base, CHUNK), b * LANES : (b + 1) * LANES] = lo
        for c in range(D3):
            lterm[pl.ds(n0, CHUNK), c * LANES : (c + 1) * LANES] = sums[c]
        return carry

    lax.fori_loop(0, SLOTS // CHUNK, step, 0)

    for m in range(4):
        load_row(m)
        hi = mix_hi[m * SLOTS : (m + 1) * SLOTS, :]
        lo = mix_lo[m * SLOTS : (m + 1) * SLOTS, :]
        part = nt(hi, midm[...]) + nt(lo, midm[...])
        for a in range(D1):
            fterm[m * PER_ROW : (m + 1) * PER_ROW, a * R : (a + 1) * R] = part[
                a * PER_ROW : (a + 1) * PER_ROW, :
            ]
        grad = tn(asub[...], hi) + tn(asub[...], lo)
        for b in range(D2):
            midf[pl.ds(b * 4 + m, R, stride=4 * D2), :] = grad[:, b * LANES : (b + 1) * LANES]
    midgrad_ref[...] = midf[...].astype(BF)

    hi, lo = split_two(fterm[...])
    first_part = tn(pick_first, hi) + tn(pick_first, lo)
    hi, lo = split_two(lterm[...])
    last_part = tn(pick_last, hi) + tn(pick_last, lo)

    @pl.when(side == 0)
    def _():
        keep_ref[...] = first_part
        send_ref[...] = last_part

    @pl.when(side != 0)
    def _():
        keep_ref[...] = last_part
        send_ref[...] = first_part


def terms(side, mine, theirs, mid):
    vmem = pl.BlockSpec(memory_space=pltpu.VMEM)
    width = D1 * R
    return pl.pallas_call(
        terms_kernel,
        out_shape=(
            jax.ShapeDtypeStruct(mid.shape, BF),
            jax.ShapeDtypeStruct((SLOTS, width), F32),
            jax.ShapeDtypeStruct((SLOTS, width), F32),
        ),
        in_specs=[pl.BlockSpec(memory_space=pltpu.SMEM)] + [vmem] * 3,
        out_specs=(vmem, vmem, vmem),
        scratch_shapes=[
            pltpu.VMEM((2, SLOTS, width), BF),
            pltpu.VMEM((SLOTS, width), BF),
            pltpu.VMEM((SLOTS, width), F32),
            pltpu.VMEM((SLOTS, LANES), F32),
            pltpu.VMEM((4 * SLOTS, D2 * R), BF),
            pltpu.VMEM((4 * SLOTS, D2 * R), BF),
            pltpu.VMEM((4 * SLOTS, D2 * R), BF),
            pltpu.VMEM((SLOTS, width), F32),
            pltpu.VMEM((SLOTS, width), F32),
            pltpu.VMEM((R, D2 * R), BF),
            pltpu.VMEM((SLOTS, R), BF),
            pltpu.VMEM(mid.shape, F32),
        ],
        interpret=INTERPRET,
        name="terms",
    )(side, mine, theirs, mid)


def outer_kernel(side_ref, mine_ref, theirs_ref, *refs):
    side = side_ref[0]
    mine, theirs = mine_ref[...], theirs_ref[...]
    first_grad = jnp.where(side == 0, mine, theirs)
    last_grad = jnp.where(side == 0, theirs, mine)
    width = mine.shape[1]
    dest = iota((width, width), 1)
    source = (dest % D3) * LANES + dest // D3
    order = ones_where(iota((width, width), 0) == source)
    hi = last_grad.astype(BF)
    rest = last_grad - hi.astype(F32)
    low, lowest = split_two(rest)
    last_grad = nn(hi, order) + (nn(low, order) + nn(lowest, order))
    f_next = adam_update(refs[0][...], refs[1][...], refs[2][...], first_grad)
    l_next = adam_update(refs[3][...], refs[4][...], refs[5][...], last_grad)
    for ref, value in zip(refs[6:], f_next + l_next):
        ref[...] = value


def outer_step(side, mine, theirs, states):
    vmem = pl.BlockSpec(memory_space=pltpu.VMEM)
    return pl.pallas_call(
        outer_kernel,
        out_shape=tuple(jax.ShapeDtypeStruct(mine.shape, F32) for _ in range(6)),
        in_specs=[pl.BlockSpec(memory_space=pltpu.SMEM)] + [vmem] * 8,
        out_specs=(vmem,) * 6,
        interpret=INTERPRET,
        name="outer",
    )(side, mine, theirs, *states)


def row_tiles(x):
    return x.reshape(4, D2 * R, LANES).transpose(1, 0, 2).reshape(4 * D2 * R, LANES)


def untile(x):
    return x.reshape(D2 * R, 4, LANES).transpose(1, 0, 2).reshape(4, D2 * R * LANES)


CORE_SWAP = ((0, 1), (1, 0), (2, 3), (3, 2))
CHIP_SWAP = ((0, 2), (2, 0), (1, 3), (3, 1))


def local(
    first_core,
    first_moment,
    first_second,
    mid_core,
    mid_moment,
    mid_second,
    last_core,
    last_moment,
    last_second,
    cotangent,
    bag_lengths,
    first_digit,
    mid_digit,
    last_digit,
):
    side = (lax.axis_index("rep") % 2).astype(jnp.int32).reshape(1)
    packed = pack(
        side,
        mid_digit.reshape(1, -1),
        first_digit.reshape(1, -1),
        last_digit.reshape(1, -1),
        bag_lengths,
        cotangent,
        first_core,
        last_core,
    )
    mine = lax.all_to_all(packed, "dp", split_axis=0, concat_axis=0, tiled=True)
    theirs = lax.ppermute(mine, "rep", CORE_SWAP)
    mid_part, keep, send = terms(side, mine, theirs, row_tiles(mid_core))

    other = lax.ppermute(send, "rep", CORE_SWAP)
    share = lax.all_to_all(
        (keep + other).astype(BF), "dp", split_axis=0, concat_axis=0, tiled=True
    )
    share = jnp.sum(share.reshape(N_SRC, -1, share.shape[1]).astype(F32), axis=0)

    half_rows = mid_part.shape[0] // 2
    mid_other = lax.ppermute(mid_part, "rep", CORE_SWAP)
    mid_chip = (mid_part.astype(F32) + mid_other.astype(F32)).astype(BF)
    half = lax.dynamic_slice_in_dim(mid_chip, side[0] * half_rows, half_rows, axis=0)
    far_half = lax.ppermute(half, "rep", CHIP_SWAP)
    far_rest = lax.ppermute(far_half, "rep", CORE_SWAP)
    far = jnp.where(
        side[0] == 0,
        jnp.concatenate([far_half, far_rest], axis=0),
        jnp.concatenate([far_rest, far_half], axis=0),
    )
    mid_grad = mid_chip.astype(F32) + far.astype(F32)
    mid_next = adam_update(row_tiles(mid_core), row_tiles(mid_moment), row_tiles(mid_second), mid_grad)
    mid_next = tuple(untile(x) for x in mid_next)

    share = share + lax.ppermute(share, "rep", CHIP_SWAP)
    other_share = lax.ppermute(share, "rep", CORE_SWAP)
    outer = outer_step(
        side,
        share,
        other_share,
        (first_core, first_moment, first_second, last_core, last_moment, last_second),
    )
    return outer[:3] + mid_next + outer[3:]


def solution(mesh):
    rows = P("dp", None)
    spread = P(("rep", "dp"), None)
    flat = P(("rep", "dp"))
    return jax.shard_map(
        local,
        mesh=mesh,
        in_specs=(rows,) * 9 + (spread, spread, flat, spread, flat),
        out_specs=(rows,) * 9,
        check_vma=False,
    )
```

time: 1320 us -> 122 us (0.09)
  waiting for transfers between devices: 744 us -> 20.1 us
  blocking collectives: 368 us -> 37.6 us
  local copies, waits for them, and re-layouts: 108 us -> 1.57 us
  Pallas kernels: 0 us -> 33.7 us
  matrix products: 32.4 us -> 0 us
  between operations: 15.7 us -> 0.74 us
    reduce_scatter x2 -> x0, waiting for transfers between devices: 733 us -> none  [the longest x1 367 us: local(): lax.psum_scatter(first_part, 'dp', scatter_dimension=0, tiled=True)]
    all_gather x2 -> x0, blocking collectives: 306 us -> none  [the longest x1 156 us: local(): lax.all_gather(last_core.astype(jnp.bfloat16), 'dp', axis=0, tiled=True)]
    psum x1 -> x0, blocking collectives: 62.4 us -> none  [local(): first_grad, last_grad = lax.psum((shares[0], shares[1]), 'rep')]
    dynamic_update_slice x12 -> x0, local copies, waits for them, and re-layouts: 45.8 us -> none  [core_terms(): lax.map(partial(slot_terms, first_copy=first_copy, last_copy=last_copy),...]
    all_to_all x0 -> x1, blocking collectives: none -> 37.6 us  [local(): mine = lax.all_to_all(packed, 'dp', split_axis=0, concat_axis=0, tiled=True)]
    pallas_call x0 -> x3, Pallas kernels: none -> 33.7 us  [the longest x1 29.5 us: terms(): pl.pallas_call(terms_kernel, out_shape=(jax.ShapeDtypeStruct(mid.shape, B...]
    dot_general x24 -> x0, matrix products: 32.4 us -> none  [the longest x4 7.35 us: slot_terms(): jnp.einsum('kabc,krbc->kar', grad_cube, tail_mix, preferred_element_type=...]
    ppermute x0 -> x7, waiting for transfers between devices: none -> 20.1 us  [the longest x1 15.8 us: local(): far_half = lax.ppermute(half, 'rep', CHIP_SWAP)]
  transfers between devices with their start and end apart: 5 -> 8, of which waited for: 3 -> 3; matrix products, arithmetic and copies ran while one was open for 1% -> 13% of each run, Pallas kernels for 0% -> 0%
where the time goes in v1:
time: 122 us
  blocking collectives  37.6 us (31%)
  Pallas kernels  33.7 us (28%)
  waiting for transfers between devices  20.1 us (16%)
  other arithmetic  15.7 us (13%)
  starting transfers between devices  12.1 us (10%)
  local copies, waits for them, and re-layouts  1.57 us (1%)
    all_to_all x1, blocking collectives, local(): mine = lax.all_to_all(packed, 'dp', split_axis=0, concat_axis=0, tiled=True)  37.6 us
    pallas_call x1, Pallas kernels, terms(): pl.pallas_call(terms_kernel, out_shape=(jax.ShapeDtypeStruct(mid.shape, B...  29.5 us
    ppermute x1, waiting for transfers between devices, local(): far_half = lax.ppermute(half, 'rep', CHIP_SWAP)  15.8 us
    sub x1, other arithmetic, adam_update(): current - LEARN_RATE * corrected / (spread + EPSILON)  6.43 us
    all_to_all x1, starting transfers between devices, local(): lax.all_to_all((keep + other).astype(BF), 'dp', split_axis=0, concat_axis...  5.89 us
    mul x1, other arithmetic, adam_update(): second_next = BETA_TWO * second + (1.0 - BETA_TWO) * gradient * gradient  3.45 us
    ppermute x1, starting transfers between devices, local(): theirs = lax.ppermute(mine, 'rep', CORE_SWAP)  2.88 us
  transfers between devices with their start and end apart: 8, of which 3 were waited for; matrix products, arithmetic and copies ran while one was open for 13% of the time, Pallas kernels for 0%

profile of v1, /device:TPU:1, one launch (start us, length us, event | category | flops | bytes accessed | tf_op | source)
XLA Modules:
  0.0 121.5 jit_solution(16279471004235503105)
XLA Ops:
  0.7 2.4 %pack.1 = bf16[512,768]{1,0:T(8,128)(2,1)} custom-call(s32[1]{0:T(128)} %bitcast.side_ref, s32[1,256]{1,0:T(1,128)} %bitcast.48, s32[1,256]{1,0:T(1,128)} %bitcast.49, s32[1,256]{1,0:T(1,128)} %bitcast.50, s32[1,16]{1,0:T(1,128)} %bag_ref.1, bf16[16,128]{1,0:T(8,128)(2,1)} %cot_ref.1, f32[8,512]{1,0:T(8,128)} %refs_0_.1, f32[8,512]{1,0:T(8,128)} %refs_3_.1), custom_call_target="tpu_custom_call" | custom-call | tf_op jit(solution)/shard_map/pack/pallas_call | solution.py:107
  3.0 37.6 %all_to_all.20 = bf16[64,8,768]{2,1,0:T(8,128)(2,1)S(1)} all-to-all(bf16[64,8,768]{2,1,0:T(8,128)(2,1)} %bitcast.42), channel_id=1, replica_groups=mesh['rep'=4,'dp'=64] {'dp'}, dimensions={0} | all-to-all | bytes 1572864 | tf_op jit(solution)/shard_map/all_to_all | solution.py:311
  40.7 2.9 %collective-permute-start = (bf16[512,768]{1,0:T(8,128)(2,1)S(1)}, bf16[512,768]{1,0:T(8,128)(2,1)S(1)}, u32[]{:S(2)}, u32[]{:S(2)}) collective-permute-start(bf16[512,768]{1,0:T(8,128)(2,1)S(1)} %bitcast.43), channel_id=1, source_target_pairs={{0,64},{64,0},{128,192},{192,128},{1,65},{65,1},{129,193},{193,129... | collective-permute-start | bytes 2359304 | tf_op jit(solution)/shard_map/ppermute | solution.py:312
  43.5 1.9 %collective-permute-done.theirs_ref = bf16[512,768]{1,0:T(8,128)(2,1)S(1)} collective-permute-done((bf16[512,768]{1,0:T(8,128)(2,1)S(1)}, bf16[512,768]{1,0:T(8,128)(2,1)S(1)}, u32[]{:S(2)}, u32[]{:S(2)}) %collective-permute-start) | collective-permute-done | bytes 786464 | tf_op jit(solution)/shard_map/ppermute | solution.py:312
  45.5 0.9 copy-done.4
  46.4 29.5 %terms.1 = (bf16[4096,128]{1,0:T(8,128)(2,1)}, f32[512,512]{1,0:T(8,128)}, f32[512,512]{1,0:T(8,128)}) custom-call(s32[1]{0:T(128)} %bitcast.side_ref, bf16[512,768]{1,0:T(8,128)(2,1)} %bitcast.44, bf16[512,768]{1,0:T(8,128)(2,1)} %copy-done.4, f32[4096,128]{1,0:T(8,128)} %bitcast.38), custom_call_target="tpu_custom_call" | custom-call | tf_op jit(solution)/shard_map/terms/pallas_call | solution.py:213
  75.9 0.3 collective-permute-start.1
  76.3 0.2 collective-permute-start.4
  76.4 2.4 %collective-permute-done.1 = f32[512,512]{1,0:T(8,128)S(1)} collective-permute-done((f32[512,512]{1,0:T(8,128)}, f32[512,512]{1,0:T(8,128)S(1)}, u32[]{:S(2)}, u32[]{:S(2)}) %collective-permute-start.1) | collective-permute-done | bytes 1048608 | tf_op jit(solution)/shard_map/ppermute | solution.py:315
  78.8 2.2 %fusion.1 = bf16[64,8,512]{2,1,0:T(8,128)(2,1)} fusion(f32[512,512]{1,0:T(8,128)} %get-tuple-element.18, f32[512,512]{1,0:T(8,128)S(1)} %collective-permute-done.1), kind=kLoop, calls=%fused_computation.11 | loop fusion | flops 524288 | bytes 2621440 | tf_op jit(solution)/shard_map/all_to_all | solution.py:316
  81.0 5.9 %all-to-all-start.1 = ((bf16[64,8,512]{2,1,0:T(8,128)(2,1)}), bf16[64,8,512]{2,1,0:T(8,128)(2,1)S(1)}, u32[]{:S(2)}, u32[]{:S(2)}) async-start(bf16[64,8,512]{2,1,0:T(8,128)(2,1)} %fusion.1), calls=%async_computation.1 | async-start | bytes 1048576 | tf_op jit(solution)/shard_map/all_to_all | solution.py:316
  86.9 0.0 copy-start.2
  86.9 1.6 %add_convert_fusion = bf16[4096,128]{1,0:T(8,128)(2,1)S(1)} fusion(bf16[4096,128]{1,0:T(8,128)(2,1)} %collective-permute-done.4, bf16[4096,128]{1,0:T(8,128)(2,1)S(1)} %copy-done.3), kind=kLoop, calls=%fused_computation.5 | loop fusion | flops 2097152 | bytes 3145728 | tf_op jit(solution)/shard_map/convert_element_type | solution.py:323
  88.6 0.5 collective-permute-start.5
  89.1 1.9 %broadcast_multiply_fusion.1 = f32[4,131072]{1,0:T(4,128)} fusion(f32[4,131072]{1,0:T(4,128)S(1)} %copy-done.2), kind=kLoop, calls=%fused_computation.8 | loop fusion | flops 524288 | bytes 4194304 | tf_op jit(solution)/shard_map/mul | solution.py:34
  90.9 15.8 %collective-permute-done.5 = bf16[2048,128]{1,0:T(8,128)(2,1)} collective-permute-done((bf16[2048,128]{1,0:T(8,128)(2,1)S(1)}, bf16[2048,128]{1,0:T(8,128)(2,1)}, u32[]{:S(2)}, u32[]{:S(2)}) %collective-permute-start.5) | collective-permute-done | bytes 524320 | tf_op jit(solution)/shard_map/ppermute | solution.py:325
  106.7 1.2 collective-permute-start.6
  107.9 0.1 convert_reduce_fusion
  108.1 0.8 collective-permute-start.2
  108.8 3.4 %broadcast_multiply_fusion = f32[4,131072]{1,0:T(4,128)} fusion(f32[4,131072]{1,0:T(4,128)} %param.19), kind=kLoop, calls=%fused_computation.7 | loop fusion | flops 524288 | bytes 4194304 | tf_op jit(solution)/shard_map/mul | solution.py:35
  112.3 0.4 collective-permute-start.3
  112.7 6.4 %divide_subtract_fusion = (f32[4096,128]{1,0:T(8,128)}, f32[4096,128]{1,0:T(8,128)}, f32[4096,128]{1,0:T(8,128)}) fusion(f32[4096,128]{1,0:T(8,128)S(1)} %bitcast.39, f32[4096,128]{1,0:T(8,128)} %bitcast.40, bf16[2048,128]{1,0:T(8,128)(2,1)} %collective-permute-done.5, bf16[2048,128]{1,0:T(8,128)(2,1)} %collective-permute-done.6, pred[]{:T(512)S(6)} %eq.5, ...), kind=kLoop, calls=%fused_computation.2 | loop fusion | flops 11534336 | bytes 14680065 | tf_op jit(solution)/shard_map/sub | solution.py:38
  119.1 0.6 copy-done.6
  119.7 1.8 %outer.1 = (f32[8,512]{1,0:T(8,128)}, f32[8,512]{1,0:T(8,128)}, f32[8,512]{1,0:T(8,128)}, f32[8,512]{1,0:T(8,128)}, f32[8,512]{1,0:T(8,128)}, /*index=5*/f32[8,512]{1,0:T(8,128)}) custom-call(s32[1]{0:T(128)} %bitcast.side_ref, f32[8,512]{1,0:T(8,128)} %copy-done.5, f32[8,512]{1,0:T(8,128)} %copy-done.6, f32[8,512]{1,0:T(8,128)} %refs_0_.1, ...), custom_call_target="tpu_custom_call" | custom-call | tf_op jit(solution)/shard_map/outer/pallas_call | solution.py:262
  (18 shorter events, 0.1 us)
Async XLA Ops:
  40.7 4.8 %copy-start.1 = (bf16[64,8,768]{2,1,0:T(8,128)(2,1)}, bf16[64,8,768]{2,1,0:T(8,128)(2,1)S(1)}, u32[]{:S(2)}) copy-start(bf16[64,8,768]{2,1,0:T(8,128)(2,1)S(1)} %all_to_all.20) | copy-start | bytes 2359300
  40.7 4.8 %collective-permute-start = (bf16[512,768]{1,0:T(8,128)(2,1)S(1)}, bf16[512,768]{1,0:T(8,128)(2,1)S(1)}, u32[]{:S(2)}, u32[]{:S(2)}) collective-permute-start(bf16[512,768]{1,0:T(8,128)(2,1)S(1)} %bitcast.43), channel_id=1, source_target_pairs={{0,64},{64,0},{128,192},{192,128},{1,65},{65,1},{129,193},{193,129... | collective-permute-start | bytes 2359304 | tf_op jit(solution)/shard_map/ppermute | solution.py:312
  45.5 0.9 copy-start.4
  75.9 11.0 %copy-start.3 = (bf16[4096,128]{1,0:T(8,128)(2,1)S(1)}, bf16[4096,128]{1,0:T(8,128)(2,1)}, u32[]{:S(2)}) copy-start(bf16[4096,128]{1,0:T(8,128)(2,1)} %get-tuple-element.23) | copy-start | bytes 3145732
  75.9 2.9 %collective-permute-start.1 = (f32[512,512]{1,0:T(8,128)}, f32[512,512]{1,0:T(8,128)S(1)}, u32[]{:S(2)}, u32[]{:S(2)}) collective-permute-start(f32[512,512]{1,0:T(8,128)} %get-tuple-element.19), channel_id=1, source_target_pairs={{0,64},{64,0},{128,192},{192,128},{1,65},{65,1},{129,193},{193,129... | collective-permute-start | bytes 3145736 | tf_op jit(solution)/shard_map/ppermute | solution.py:315
  76.3 10.6 %collective-permute-start.4 = (bf16[4096,128]{1,0:T(8,128)(2,1)}, bf16[4096,128]{1,0:T(8,128)(2,1)}, u32[]{:S(2)}, u32[]{:S(2)}) collective-permute-start(bf16[4096,128]{1,0:T(8,128)(2,1)} %get-tuple-element.23), channel_id=1, source_target_pairs={{0,64},{64,0},{128,192},{192,128},{1,65},{65,1},{129,193},{193,129... | collective-permute-start | bytes 3145736 | tf_op jit(solution)/shard_map/ppermute | solution.py:322
  81.0 27.0 %all-to-all-start.1 = ((bf16[64,8,512]{2,1,0:T(8,128)(2,1)}), bf16[64,8,512]{2,1,0:T(8,128)(2,1)S(1)}, u32[]{:S(2)}, u32[]{:S(2)}) async-start(bf16[64,8,512]{2,1,0:T(8,128)(2,1)} %fusion.1), calls=%async_computation.1 | async-start | bytes 1048576 | tf_op jit(solution)/shard_map/all_to_all | solution.py:316
  86.9 2.2 %copy-start.2 = (f32[4,131072]{1,0:T(4,128)S(1)}, f32[4,131072]{1,0:T(4,128)}, u32[]{:S(2)}) copy-start(f32[4,131072]{1,0:T(4,128)} %param.18) | copy-start | bytes 6291460
  88.6 18.2 %collective-permute-start.5 = (bf16[2048,128]{1,0:T(8,128)(2,1)S(1)}, bf16[2048,128]{1,0:T(8,128)(2,1)}, u32[]{:S(2)}, u32[]{:S(2)}) collective-permute-start(bf16[2048,128]{1,0:T(8,128)(2,1)S(1)} %constant_dynamic-slice_fusion), channel_id=1, source_target_pairs={{0,128},{128,0},{64,192},{192,64},{1,129},{129,1},{65,193},{193,65... | collective-permute-start | bytes 1572872 | tf_op jit(solution)/shard_map/ppermute | solution.py:325
  106.7 5.9 %collective-permute-start.6 = (bf16[2048,128]{1,0:T(8,128)(2,1)}, bf16[2048,128]{1,0:T(8,128)(2,1)}, u32[]{:S(2)}, u32[]{:S(2)}) collective-permute-start(bf16[2048,128]{1,0:T(8,128)(2,1)} %collective-permute-done.5), channel_id=1, source_target_pairs={{0,64},{64,0},{128,192},{192,128},{1,65},{65,1},{129,193},{193,129... | collective-permute-start | bytes 1572872 | tf_op jit(solution)/shard_map/ppermute | solution.py:326
  108.0 4.6 %copy-start = (f32[4,131072]{1,0:T(4,128)S(1)}, f32[4,131072]{1,0:T(4,128)}, u32[]{:S(2)}) copy-start(f32[4,131072]{1,0:T(4,128)} %param.17) | copy-start | bytes 6291460
  108.1 4.2 %collective-permute-start.2 = (f32[8,512]{1,0:T(8,128)S(1)}, f32[8,512]{1,0:T(8,128)S(1)}, u32[]{:S(2)}, u32[]{:S(2)}) collective-permute-start(f32[8,512]{1,0:T(8,128)S(1)} %convert_reduce_fusion), channel_id=1, source_target_pairs={{0,128},{128,0},{64,192},{192,64},{1,129},{129,1},{65,193},{193,65... | collective-permute-start | bytes 49160 | tf_op jit(solution)/shard_map/ppermute | solution.py:336
  112.3 6.8 %copy-start.5 = (f32[8,512]{1,0:T(8,128)}, f32[8,512]{1,0:T(8,128)S(1)}, u32[]{:S(2)}) copy-start(f32[8,512]{1,0:T(8,128)S(1)} %add.33.mine_ref) | copy-start | bytes 49156
  112.3 6.8 %collective-permute-start.3 = (f32[8,512]{1,0:T(8,128)S(1)}, f32[8,512]{1,0:T(8,128)S(1)}, u32[]{:S(2)}, u32[]{:S(2)}) collective-permute-start(f32[8,512]{1,0:T(8,128)S(1)} %add.33.mine_ref), channel_id=1, source_target_pairs={{0,64},{64,0},{128,192},{192,128},{1,65},{65,1},{129,193},{193,129... | collective-permute-start | bytes 49160 | tf_op jit(solution)/shard_map/ppermute | solution.py:337
  119.1 0.6 copy-start.6

commit v2 on v1

--- a/solution.py
+++ b/solution.py
@@ -1,5 +1,3 @@
-from functools import partial
-
 import jax
 import jax.numpy as jnp
 from jax import lax
@@ -7,7 +5,7 @@
 from jax.experimental.pallas import tpu as pltpu
 from jax.sharding import PartitionSpec as P
 
-N2 = 256
+
 R = 128
 D1 = 4
 D2 = 8
@@ -17,8 +15,7 @@
 LANES = 128
 N_SRC = 64
 SLOTS = 512
-PER_ROW = 128
-CHUNK = 16
+GROUP = 64
 
 LEARN_RATE = 0.01
 BETA_ONE = 0.9
@@ -117,83 +114,105 @@
 def terms_kernel(
     side_ref, mine_ref, theirs_ref, mid_ref,
     midgrad_ref, keep_ref, send_ref,
-    cores, arows, lrows, grads, head, mix_hi, mix_lo, fterm, lterm, midm, asub, midf,
+    cores, lrows, pick, diag, mix_hi, mix_lo, fterm, lterm, midm, asub, midf,
 ):
     side = side_ref[0]
-    width = cores.shape[2]
     cores[side] = mine_ref[:, 2 * LANES :]
     cores[1 - side] = theirs_ref[:, 2 * LANES :]
-    new = iota((SLOTS, SLOTS), 0)
-    old = (new % 64) * 8 + (new // 128) * 2 + (new // 64) % 2
-    lane = iota((SLOTS, SLOTS), 1)
-    slots = nn(ones_where(lane == old), mine_ref[:, 0 : 2 * LANES])
-    grads[...] = slots[:, 0:LANES]
+    up, across = iota((SLOTS, SLOTS), 0), iota((SLOTS, SLOTS), 1)
+    slots = nn(ones_where(across == (up % GROUP) * 8 + up // GROUP), mine_ref[:, 0 : 2 * LANES])
+    grads = slots[:, 0:LANES].astype(BF)
     first = slots[:, LANES : LANES + 1] * 32.0 + slots[:, LANES + 1 : LANES + 2]
     last = slots[:, LANES + 2 : LANES + 3] * 32.0 + slots[:, LANES + 3 : LANES + 4]
-    lane_f = lane.astype(F32)
-    pick_first = ones_where(lane_f == first)
-    pick_last = ones_where(lane_f == last)
-    arows[...] = nn(pick_first, cores[0]).astype(BF)
-    lrows[...] = nn(pick_last, cores[1])
-
-    def load_row(m):
+    across_f = across.astype(F32)
+    pick_first = ones_where(across_f == first)
+    pick_last = ones_where(across_f == last)
+    arows = nn(pick_first, cores[0]).astype(BF)
+    last_rows = nn(pick_last, cores[1]).astype(BF)
+    for q in range(8):
+        for c in range(D3):
+            lrows[q, c * GROUP : (c + 1) * GROUP, :] = last_rows[
+                q * GROUP : (q + 1) * GROUP, c * LANES : (c + 1) * LANES
+            ]
+        for a in range(D1):
+            asub[q, a * GROUP : (a + 1) * GROUP, :] = arows[
+                q * GROUP : (q + 1) * GROUP, a * R : (a + 1) * R
+            ]
+
+    pick[...] = jnp.zeros(pick.shape, BF)
+    tile_row, tile_lane = iota((16, LANES), 0), iota((16, LANES), 1)
+    for i in range(2 * D1 * D2):
+        pick[i, (i // 8) * 16 : (i // 8) * 16 + 16, :] = ones_where(
+            tile_row == 2 * (i % 8) + tile_lane // GROUP
+        )
+    own = ones_where(iota((SLOTS, 2 * LANES), 0) % GROUP == iota((SLOTS, 2 * LANES), 1) % GROUP)
+
+    def spread(ab, carry):
+        pair = jnp.concatenate([pick[2 * ab], pick[2 * ab + 1]], axis=1)
+        value = nn(grads, pair).astype(BF) * own
+        diag[0, ab] = value[:, 0:LANES]
+        diag[1, ab] = value[:, LANES:]
+        return carry
+
+    lax.fori_loop(0, D1 * D2, spread, 0)
+
+    for m in range(4):
         for b in range(D2):
-            midm[:, b * LANES : (b + 1) * LANES] = mid_ref[
-                pl.ds(b * 4 + m, R, stride=4 * D2), :
-            ].astype(BF)
-        for a in range(D1):
-            asub[a * PER_ROW : (a + 1) * PER_ROW, :] = arows[
-                m * PER_ROW : (m + 1) * PER_ROW, a * R : (a + 1) * R
-            ]
+            midm[m, b] = mid_ref[pl.ds(b * 4 + m, R, stride=4 * D2), :].astype(BF)
+
+    def group(q, carry):
+        here = pl.ds(pl.multiple_of(q * GROUP, GROUP), GROUP)
+        m = q // 2
+        left = asub[q]
+        weights = lrows[q]
+        total = None
+        for b in range(D2):
+            head = lax.dot_general(
+                midm[m, b], left, (((0,), (1,)), ((), ())), preferred_element_type=F32
+            ).astype(BF)
+            block = jnp.concatenate(
+                [
+                    jnp.concatenate([diag[h, a * D2 + b, here, :] for a in range(D1)], axis=0)
+                    for h in range(2)
+                ],
+                axis=1,
+            )
+            part = nn(head, block)
+            total = part if total is None else total + part
+            hi, lo = split_two(nn(block, weights))
+            there = pl.ds(pl.multiple_of(q * D1 * GROUP, D1 * GROUP), D1 * GROUP)
+            mix_hi[b, there, :] = hi
+            mix_lo[b, there, :] = lo
+        total = total.T
+        for c in range(D3):
+            lterm[c, here, :] = total[c * GROUP : (c + 1) * GROUP, :]
+        return carry
+
+    lax.fori_loop(0, 8, group, 0)
 
     for m in range(4):
-        load_row(m)
-        head[m * SLOTS : (m + 1) * SLOTS, :] = nn(asub[...], midm[...]).astype(BF)
-
-    def step(t, carry):
-        n0 = pl.multiple_of(t * CHUNK, CHUNK)
-        m = t // (PER_ROW // CHUNK)
-        k0 = n0 - m * PER_ROW
-        g = grads[pl.ds(n0, CHUNK), :]
-        rows = [lrows[pl.ds(n0, CHUNK), c * LANES : (c + 1) * LANES] for c in range(D3)]
-        sums = [jnp.zeros((CHUNK, LANES), F32) for _ in range(D3)]
-        for a in range(D1):
-            base = pl.multiple_of(m * SLOTS + a * PER_ROW + k0, CHUNK)
-            for b in range(D2):
-                at = a * D2 * D3 + b * D3
-                h = head[pl.ds(base, CHUNK), b * LANES : (b + 1) * LANES].astype(F32)
-                mix = None
-                for c in range(D3):
-                    spread = jnp.broadcast_to(g[:, at + c : at + c + 1], (CHUNK, LANES))
-                    part = spread * rows[c]
-                    mix = part if mix is None else mix + part
-                    sums[c] = sums[c] + spread * h
-                hi, lo = split_two(mix)
-                mix_hi[pl.ds(base, CHUNK), b * LANES : (b + 1) * LANES] = hi
-                mix_lo[pl.ds(base, CHUNK), b * LANES : (b + 1) * LANES] = lo
-        for c in range(D3):
-            lterm[pl.ds(n0, CHUNK), c * LANES : (c + 1) * LANES] = sums[c]
-        return carry
-
-    lax.fori_loop(0, SLOTS // CHUNK, step, 0)
-
-    for m in range(4):
-        load_row(m)
-        hi = mix_hi[m * SLOTS : (m + 1) * SLOTS, :]
-        lo = mix_lo[m * SLOTS : (m + 1) * SLOTS, :]
-        part = nt(hi, midm[...]) + nt(lo, midm[...])
-        for a in range(D1):
-            fterm[m * PER_ROW : (m + 1) * PER_ROW, a * R : (a + 1) * R] = part[
-                a * PER_ROW : (a + 1) * PER_ROW, :
-            ]
-        grad = tn(asub[...], hi) + tn(asub[...], lo)
-        for b in range(D2):
-            midf[pl.ds(b * 4 + m, R, stride=4 * D2), :] = grad[:, b * LANES : (b + 1) * LANES]
+        span = slice(m * SLOTS, (m + 1) * SLOTS)
+        left = jnp.concatenate([asub[2 * m], asub[2 * m + 1]], axis=0)
+        part = None
+        for b in range(0, D2, 2):
+            hi = jnp.concatenate([mix_hi[b, span, :], mix_hi[b + 1, span, :]], axis=1)
+            lo = jnp.concatenate([mix_lo[b, span, :], mix_lo[b + 1, span, :]], axis=1)
+            pair = jnp.concatenate([midm[m, b], midm[m, b + 1]], axis=1)
+            term = nt(jnp.concatenate([hi, lo], axis=1), jnp.concatenate([pair, pair], axis=1))
+            part = term if part is None else part + term
+            grad = tn(left, hi) + tn(left, lo)
+            midf[pl.ds(b * 4 + m, R, stride=4 * D2), :] = grad[:, 0:LANES]
+            midf[pl.ds((b + 1) * 4 + m, R, stride=4 * D2), :] = grad[:, LANES:]
+        for q in range(2):
+            for a in range(D1):
+                fterm[a, (2 * m + q) * GROUP : (2 * m + q + 1) * GROUP, :] = part[
+                    (q * D1 + a) * GROUP : (q * D1 + a + 1) * GROUP, :
+                ]
     midgrad_ref[...] = midf[...].astype(BF)
 
-    hi, lo = split_two(fterm[...])
+    hi, lo = split_two(jnp.concatenate([fterm[a] for a in range(D1)], axis=1))
     first_part = tn(pick_first, hi) + tn(pick_first, lo)
-    hi, lo = split_two(lterm[...])
+    hi, lo = split_two(jnp.concatenate([lterm[c] for c in range(D3)], axis=1))
     last_part = tn(pick_last, hi) + tn(pick_last, lo)
 
     @pl.when(side == 0)
@@ -221,16 +240,15 @@
         out_specs=(vmem, vmem, vmem),
         scratch_shapes=[
             pltpu.VMEM((2, SLOTS, width), BF),
-            pltpu.VMEM((SLOTS, width), BF),
-            pltpu.VMEM((SLOTS, width), F32),
-            pltpu.VMEM((SLOTS, LANES), F32),
-            pltpu.VMEM((4 * SLOTS, D2 * R), BF),
-            pltpu.VMEM((4 * SLOTS, D2 * R), BF),
-            pltpu.VMEM((4 * SLOTS, D2 * R), BF),
-            pltpu.VMEM((SLOTS, width), F32),
-            pltpu.VMEM((SLOTS, width), F32),
-            pltpu.VMEM((R, D2 * R), BF),
-            pltpu.VMEM((SLOTS, R), BF),
+            pltpu.VMEM((8, D3 * GROUP, LANES), BF),
+            pltpu.VMEM((2 * D1 * D2, LANES, LANES), BF),
+            pltpu.VMEM((2, D1 * D2, SLOTS, LANES), BF),
+            pltpu.VMEM((D2, 4 * SLOTS, LANES), BF),
+            pltpu.VMEM((D2, 4 * SLOTS, LANES), BF),
+            pltpu.VMEM((D1, SLOTS, LANES), F32),
+            pltpu.VMEM((D3, SLOTS, LANES), F32),
+            pltpu.VMEM((4, D2, R, LANES), BF),
+            pltpu.VMEM((8, D1 * GROUP, R), BF),
             pltpu.VMEM(mid.shape, F32),
         ],
         interpret=INTERPRET,
@@ -312,17 +330,14 @@
     theirs = lax.ppermute(mine, "rep", CORE_SWAP)
     mid_part, keep, send = terms(side, mine, theirs, row_tiles(mid_core))
 
+    mid_other = lax.ppermute(mid_part, "rep", CORE_SWAP)
     other = lax.ppermute(send, "rep", CORE_SWAP)
-    share = lax.all_to_all(
-        (keep + other).astype(BF), "dp", split_axis=0, concat_axis=0, tiled=True
-    )
-    share = jnp.sum(share.reshape(N_SRC, -1, share.shape[1]).astype(F32), axis=0)
-
     half_rows = mid_part.shape[0] // 2
-    mid_other = lax.ppermute(mid_part, "rep", CORE_SWAP)
     mid_chip = (mid_part.astype(F32) + mid_other.astype(F32)).astype(BF)
     half = lax.dynamic_slice_in_dim(mid_chip, side[0] * half_rows, half_rows, axis=0)
+    half, chip_sum = lax.optimization_barrier((half, (keep + other).astype(BF)))
     far_half = lax.ppermute(half, "rep", CHIP_SWAP)
+    share = lax.all_to_all(chip_sum, "dp", split_axis=0, concat_axis=0, tiled=True)
     far_rest = lax.ppermute(far_half, "rep", CORE_SWAP)
     far = jnp.where(
         side[0] == 0,
@@ -331,7 +346,9 @@
     )
     mid_grad = mid_chip.astype(F32) + far.astype(F32)
     mid_next = adam_update(row_tiles(mid_core), row_tiles(mid_moment), row_tiles(mid_second), mid_grad)
+    share, *mid_next = lax.optimization_barrier((share, *mid_next))
     mid_next = tuple(untile(x) for x in mid_next)
+    share = jnp.sum(share.reshape(N_SRC, -1, share.shape[1]).astype(F32), axis=0)
 
     share = share + lax.ppermute(share, "rep", CHIP_SWAP)
     other_share = lax.ppermute(share, "rep", CORE_SWAP)

time: 122 us -> 134 us (1.098)
  waiting for transfers between devices: 20.1 us -> 29.2 us
  starting transfers between devices: 12.1 us -> 15.2 us
  other arithmetic: 15.7 us -> 13.8 us
    all_to_all x1, waiting for transfers between devices: 0.01 us -> 11.2 us  [local(): lax.all_to_all(chip_sum, 'dp', split_axis=0, concat_axis=0, tiled=True)]
    ppermute x1, waiting for transfers between devices: 15.8 us -> 10.6 us  [local(): far_half = lax.ppermute(half, 'rep', CHIP_SWAP)]
    ppermute x1, starting transfers between devices: 0.37 us -> 3.54 us  [local(): other_share = lax.ppermute(share, 'rep', CORE_SWAP)]
    ppermute x1, waiting for transfers between devices: 2.36 us -> 0.01 us  [local(): other = lax.ppermute(send, 'rep', CORE_SWAP)]
    ppermute x1, waiting for transfers between devices: 0.01 us -> 2.36 us  [local(): mid_other = lax.ppermute(mid_part, 'rep', CORE_SWAP)]
    ppermute x1, waiting for transfers between devices: 0.01 us -> 2.19 us  [local(): share = share + lax.ppermute(share, 'rep', CHIP_SWAP)]
    all_to_all x1 -> x0, other arithmetic: 2.17 us -> none  [local(): lax.all_to_all((keep + other).astype(BF), 'dp', split_axis=0, concat_axis...]
    mul x1, other arithmetic: 3.45 us -> 1.86 us  [adam_update(): second_next = BETA_TWO * second + (1.0 - BETA_TWO) * gradient * gradient]
  transfers between devices with their start and end apart: 8 -> 8, of which waited for: 3 -> 6; matrix products, arithmetic and copies ran while one was open for 13% -> 9% of each run, Pallas kernels for 0% -> 0%
where the time goes in v2:
time: 134 us; the launch traced here: 133 us
  blocking collectives  37.6 us (28%)
  Pallas kernels  34.9 us (26%)
  waiting for transfers between devices  29.2 us (22%)
  starting transfers between devices  15.2 us (11%)
  other arithmetic  13.8 us (10%)
  local copies, waits for them, and re-layouts  1.93 us (1%)
    all_to_all x1, blocking collectives, local(): mine = lax.all_to_all(packed, 'dp', split_axis=0, concat_axis=0, tiled=True)  37.6 us
    pallas_call x1, Pallas kernels, terms(): pl.pallas_call(terms_kernel, out_shape=(jax.ShapeDtypeStruct(mid.shape, B...  30.7 us
    all_to_all x1, waiting for transfers between devices, local(): lax.all_to_all(chip_sum, 'dp', split_axis=0, concat_axis=0, tiled=True)  11.2 us
    ppermute x1, waiting for transfers between devices, local(): far_half = lax.ppermute(half, 'rep', CHIP_SWAP)  10.6 us
    sub x1, other arithmetic, adam_update(): current - LEARN_RATE * corrected / (spread + EPSILON)  6.45 us
    all_to_all x1, starting transfers between devices, local(): lax.all_to_all(chip_sum, 'dp', split_axis=0, concat_axis=0, tiled=True)  6.13 us
    ppermute x1, starting transfers between devices, local(): other_share = lax.ppermute(share, 'rep', CORE_SWAP)  3.54 us
    ppermute x1, starting transfers between devices, local(): theirs = lax.ppermute(mine, 'rep', CORE_SWAP)  2.88 us
  transfers between devices with their start and end apart: 8, of which 6 were waited for; matrix products, arithmetic and copies ran while one was open for 9% of the time, Pallas kernels for 0%

profile of v2, /device:TPU:1, one launch (start us, length us, event | category | flops | bytes accessed | tf_op | source)
XLA Modules:
  0.0 133.2 jit_solution(7095551354561340854)
XLA Ops:
  0.7 2.4 %pack.1 = bf16[512,768]{1,0:T(8,128)(2,1)} custom-call(s32[1]{0:T(128)} %bitcast.side_ref, s32[1,256]{1,0:T(1,128)} %bitcast.52, s32[1,256]{1,0:T(1,128)} %bitcast.53, s32[1,256]{1,0:T(1,128)} %bitcast.54, s32[1,16]{1,0:T(1,128)} %bag_ref.1, bf16[16,128]{1,0:T(8,128)(2,1)} %cot_ref.1, f32[8,512]{1,0:T(8,128)} %refs_0_.1, f32[8,512]{1,0:T(8,128)} %refs_3_.1), custom_call_target="tpu_custom_call" | custom-call | tf_op jit(solution)/shard_map/pack/pallas_call | solution.py:104
  3.0 37.6 %all_to_all.23 = bf16[64,8,768]{2,1,0:T(8,128)(2,1)S(1)} all-to-all(bf16[64,8,768]{2,1,0:T(8,128)(2,1)} %bitcast.45), channel_id=1, replica_groups=mesh['rep'=4,'dp'=64] {'dp'}, dimensions={0} | all-to-all | bytes 1572864 | tf_op jit(solution)/shard_map/all_to_all | solution.py:329
  40.7 2.9 %collective-permute-start = (bf16[512,768]{1,0:T(8,128)(2,1)S(1)}, bf16[512,768]{1,0:T(8,128)(2,1)S(1)}, u32[]{:S(2)}, u32[]{:S(2)}) collective-permute-start(bf16[512,768]{1,0:T(8,128)(2,1)S(1)} %bitcast.46), channel_id=1, source_target_pairs={{0,64},{64,0},{128,192},{192,128},{1,65},{65,1},{129,193},{193,129... | collective-permute-start | bytes 2359304 | tf_op jit(solution)/shard_map/ppermute | solution.py:330
  43.5 1.9 %collective-permute-done.theirs_ref = bf16[512,768]{1,0:T(8,128)(2,1)S(1)} collective-permute-done((bf16[512,768]{1,0:T(8,128)(2,1)S(1)}, bf16[512,768]{1,0:T(8,128)(2,1)S(1)}, u32[]{:S(2)}, u32[]{:S(2)}) %collective-permute-start) | collective-permute-done | bytes 786464 | tf_op jit(solution)/shard_map/ppermute | solution.py:330
  45.5 0.9 copy-done.5
  46.4 30.7 %terms.1 = (bf16[4096,128]{1,0:T(8,128)(2,1)}, f32[512,512]{1,0:T(8,128)}, f32[512,512]{1,0:T(8,128)}) custom-call(s32[1]{0:T(128)} %bitcast.side_ref, bf16[512,768]{1,0:T(8,128)(2,1)} %bitcast.47, bf16[512,768]{1,0:T(8,128)(2,1)} %copy-done.5, f32[4096,128]{1,0:T(8,128)} %bitcast.41), custom_call_target="tpu_custom_call" | custom-call | tf_op jit(solution)/shard_map/terms/pallas_call | solution.py:232
  77.6 2.4 %collective-permute-done.1 = bf16[4096,128]{1,0:T(8,128)(2,1)S(1)} collective-permute-done((bf16[4096,128]{1,0:T(8,128)(2,1)}, bf16[4096,128]{1,0:T(8,128)(2,1)S(1)}, u32[]{:S(2)}, u32[]{:S(2)}) %collective-permute-start.1) | collective-permute-done | bytes 1048608 | tf_op jit(solution)/shard_map/ppermute | solution.py:333
  79.9 1.5 %add_convert_fusion = bf16[4096,128]{1,0:T(8,128)(2,1)S(1)} fusion(bf16[4096,128]{1,0:T(8,128)(2,1)S(1)} %collective-permute-done.1, bf16[4096,128]{1,0:T(8,128)(2,1)} %get-tuple-element.24), kind=kLoop, calls=%fused_computation.5 | loop fusion | flops 2097152 | bytes 3145728 | tf_op jit(solution)/shard_map/convert_element_type | solution.py:336
  81.5 0.9 add_convert_fusion.1
  82.5 0.4 collective-permute-start.3
  83.2 1.9 %broadcast_multiply_fusion.1 = f32[4,131072]{1,0:T(4,128)} fusion(f32[4,131072]{1,0:T(4,128)S(1)} %copy-done.2), kind=kLoop, calls=%fused_computation.9 | loop fusion | flops 524288 | bytes 4194304 | tf_op jit(solution)/shard_map/mul | solution.py:31
  85.1 10.6 %collective-permute-done.3 = bf16[2048,128]{1,0:T(8,128)(2,1)} collective-permute-done((bf16[2048,128]{1,0:T(8,128)(2,1)S(1)}, bf16[2048,128]{1,0:T(8,128)(2,1)}, u32[]{:S(2)}, u32[]{:S(2)}) %collective-permute-start.3) | collective-permute-done | bytes 524320 | tf_op jit(solution)/shard_map/ppermute | solution.py:339
  95.7 1.2 collective-permute-start.4
  96.9 1.9 %broadcast_multiply_fusion = f32[4,131072]{1,0:T(4,128)} fusion(f32[4,131072]{1,0:T(4,128)S(1)} %copy-done.3), kind=kLoop, calls=%fused_computation.8 | loop fusion | flops 524288 | bytes 4194304 | tf_op jit(solution)/shard_map/mul | solution.py:32
  98.8 6.1 %all-to-all-start.1 = ((bf16[64,8,512]{2,1,0:T(8,128)(2,1)}), bf16[64,8,512]{2,1,0:T(8,128)(2,1)}, u32[]{:S(2)}, u32[]{:S(2)}) async-start(bf16[64,8,512]{2,1,0:T(8,128)(2,1)} %bitcast.48), calls=%async_computation.1 | async-start | bytes 1048576 | tf_op jit(solution)/shard_map/all_to_all | solution.py:340
  104.9 6.5 %divide_subtract_fusion = (f32[4096,128]{1,0:T(8,128)}, f32[4096,128]{1,0:T(8,128)}, f32[4096,128]{1,0:T(8,128)}) fusion(f32[4096,128]{1,0:T(8,128)S(1)} %bitcast.42, f32[4096,128]{1,0:T(8,128)} %bitcast.43, bf16[2048,128]{1,0:T(8,128)(2,1)} %collective-permute-done.3, bf16[2048,128]{1,0:T(8,128)(2,1)} %collective-permute-done.4, pred[]{:T(512)S(6)} %eq.5, ...), kind=kLoop, calls=%fused_computation.2 | loop fusion | flops 11534336 | bytes 14680065 | tf_op jit(solution)/shard_map/sub | solution.py:35
  111.4 11.2 %all-to-all-done.1 = bf16[64,8,512]{2,1,0:T(8,128)(2,1)} async-done(((bf16[64,8,512]{2,1,0:T(8,128)(2,1)}), bf16[64,8,512]{2,1,0:T(8,128)(2,1)}, u32[]{:S(2)}, u32[]{:S(2)}) %all-to-all-start.1) | async-done | bytes 524320 | tf_op jit(solution)/shard_map/all_to_all | solution.py:340
  122.6 1.1 convert_reduce_fusion
  123.8 0.5 collective-permute-start.5
  124.2 2.2 %collective-permute-done.5 = f32[8,512]{1,0:T(8,128)S(1)} collective-permute-done((f32[8,512]{1,0:T(8,128)S(1)}, f32[8,512]{1,0:T(8,128)S(1)}, u32[]{:S(2)}, u32[]{:S(2)}) %collective-permute-start.5) | collective-permute-done | bytes 16416 | tf_op jit(solution)/shard_map/ppermute | solution.py:353
  126.4 3.5 %collective-permute-start.6 = (f32[8,512]{1,0:T(8,128)S(1)}, f32[8,512]{1,0:T(8,128)S(1)}, u32[]{:S(2)}, u32[]{:S(2)}) collective-permute-start(f32[8,512]{1,0:T(8,128)S(1)} %add.40.mine_ref), channel_id=1, source_target_pairs={{0,64},{64,0},{128,192},{192,128},{1,65},{65,1},{129,193},{193,129... | collective-permute-start | bytes 49160 | tf_op jit(solution)/shard_map/ppermute | solution.py:354
  130.0 0.8 collective-permute-done.6.theirs_ref
  130.8 0.6 copy-done.7
  131.4 1.8 %outer.1 = (f32[8,512]{1,0:T(8,128)}, f32[8,512]{1,0:T(8,128)}, f32[8,512]{1,0:T(8,128)}, f32[8,512]{1,0:T(8,128)}, f32[8,512]{1,0:T(8,128)}, /*index=5*/f32[8,512]{1,0:T(8,128)}) custom-call(s32[1]{0:T(128)} %bitcast.side_ref, f32[8,512]{1,0:T(8,128)} %copy-done.6, f32[8,512]{1,0:T(8,128)} %copy-done.7, f32[8,512]{1,0:T(8,128)} %refs_0_.1, ...), custom_call_target="tpu_custom_call" | custom-call | tf_op jit(solution)/shard_map/outer/pallas_call | solution.py:280
  (20 shorter events, 0.9 us)
Async XLA Ops:
  40.7 4.8 %copy-start.1 = (bf16[64,8,768]{2,1,0:T(8,128)(2,1)}, bf16[64,8,768]{2,1,0:T(8,128)(2,1)S(1)}, u32[]{:S(2)}) copy-start(bf16[64,8,768]{2,1,0:T(8,128)(2,1)S(1)} %all_to_all.23) | copy-start | bytes 2359300
  40.7 4.8 %collective-permute-start = (bf16[512,768]{1,0:T(8,128)(2,1)S(1)}, bf16[512,768]{1,0:T(8,128)(2,1)S(1)}, u32[]{:S(2)}, u32[]{:S(2)}) collective-permute-start(bf16[512,768]{1,0:T(8,128)(2,1)S(1)} %bitcast.46), channel_id=1, source_target_pairs={{0,64},{64,0},{128,192},{192,128},{1,65},{65,1},{129,193},{193,129... | collective-permute-start | bytes 2359304 | tf_op jit(solution)/shard_map/ppermute | solution.py:330
  45.5 0.9 copy-start.5
  77.0 2.9 %collective-permute-start.1 = (bf16[4096,128]{1,0:T(8,128)(2,1)}, bf16[4096,128]{1,0:T(8,128)(2,1)S(1)}, u32[]{:S(2)}, u32[]{:S(2)}) collective-permute-start(bf16[4096,128]{1,0:T(8,128)(2,1)} %get-tuple-element.24), channel_id=1, source_target_pairs={{0,64},{64,0},{128,192},{192,128},{1,65},{65,1},{129,193},{193,129... | collective-permute-start | bytes 3145736 | tf_op jit(solution)/shard_map/ppermute | solution.py:333
  77.4 4.1 %copy-start.4 = (f32[512,512]{1,0:T(8,128)S(1)}, f32[512,512]{1,0:T(8,128)}, u32[]{:S(2)}) copy-start(f32[512,512]{1,0:T(8,128)} %get-tuple-element.25) | copy-start | bytes 3145732
  77.4 4.1 %collective-permute-start.2 = (f32[512,512]{1,0:T(8,128)}, f32[512,512]{1,0:T(8,128)S(1)}, u32[]{:S(2)}, u32[]{:S(2)}) collective-permute-start(f32[512,512]{1,0:T(8,128)} %get-tuple-element.26), channel_id=1, source_target_pairs={{0,64},{64,0},{128,192},{192,128},{1,65},{65,1},{129,193},{193,129... | collective-permute-start | bytes 3145736 | tf_op jit(solution)/shard_map/ppermute | solution.py:334
  81.4 1.8 %copy-start.2 = (f32[4,131072]{1,0:T(4,128)S(1)}, f32[4,131072]{1,0:T(4,128)}, u32[]{:S(2)}) copy-start(f32[4,131072]{1,0:T(4,128)} %param.18) | copy-start | bytes 6291460
  82.5 14.4 %copy-start.3 = (f32[4,131072]{1,0:T(4,128)S(1)}, f32[4,131072]{1,0:T(4,128)}, u32[]{:S(2)}) copy-start(f32[4,131072]{1,0:T(4,128)} %param.19) | copy-start | bytes 6291460
  82.5 13.2 %collective-permute-start.3 = (bf16[2048,128]{1,0:T(8,128)(2,1)S(1)}, bf16[2048,128]{1,0:T(8,128)(2,1)}, u32[]{:S(2)}, u32[]{:S(2)}) collective-permute-start(bf16[2048,128]{1,0:T(8,128)(2,1)S(1)} %constant_dynamic-slice_fusion), channel_id=1, source_target_pairs={{0,128},{128,0},{64,192},{192,64},{1,129},{129,1},{65,193},{193,65... | collective-permute-start | bytes 1572872 | tf_op jit(solution)/shard_map/ppermute | solution.py:339
  85.1 19.9 %copy-start = (f32[4,131072]{1,0:T(4,128)S(1)}, f32[4,131072]{1,0:T(4,128)}, u32[]{:S(2)}) copy-start(f32[4,131072]{1,0:T(4,128)} %param.17) | copy-start | bytes 6291460
  95.7 9.2 %collective-permute-start.4 = (bf16[2048,128]{1,0:T(8,128)(2,1)}, bf16[2048,128]{1,0:T(8,128)(2,1)}, u32[]{:S(2)}, u32[]{:S(2)}) collective-permute-start(bf16[2048,128]{1,0:T(8,128)(2,1)} %collective-permute-done.3), channel_id=1, source_target_pairs={{0,64},{64,0},{128,192},{192,128},{1,65},{65,1},{129,193},{193,129... | collective-permute-start | bytes 1572872 | tf_op jit(solution)/shard_map/ppermute | solution.py:341
  98.8 23.9 %all-to-all-start.1 = ((bf16[64,8,512]{2,1,0:T(8,128)(2,1)}), bf16[64,8,512]{2,1,0:T(8,128)(2,1)}, u32[]{:S(2)}, u32[]{:S(2)}) async-start(bf16[64,8,512]{2,1,0:T(8,128)(2,1)} %bitcast.48), calls=%async_computation.1 | async-start | bytes 1048576 | tf_op jit(solution)/shard_map/all_to_all | solution.py:340
  123.8 2.7 %collective-permute-start.5 = (f32[8,512]{1,0:T(8,128)S(1)}, f32[8,512]{1,0:T(8,128)S(1)}, u32[]{:S(2)}, u32[]{:S(2)}) collective-permute-start(f32[8,512]{1,0:T(8,128)S(1)} %convert_reduce_fusion), channel_id=1, source_target_pairs={{0,128},{128,0},{64,192},{192,64},{1,129},{129,1},{65,193},{193,65... | collective-permute-start | bytes 49160 | tf_op jit(solution)/shard_map/ppermute | solution.py:353
  126.4 4.4 %copy-start.6 = (f32[8,512]{1,0:T(8,128)}, f32[8,512]{1,0:T(8,128)S(1)}, u32[]{:S(2)}) copy-start(f32[8,512]{1,0:T(8,128)S(1)} %add.40.mine_ref) | copy-start | bytes 49156
  126.4 4.4 %collective-permute-start.6 = (f32[8,512]{1,0:T(8,128)S(1)}, f32[8,512]{1,0:T(8,128)S(1)}, u32[]{:S(2)}, u32[]{:S(2)}) collective-permute-start(f32[8,512]{1,0:T(8,128)S(1)} %add.40.mine_ref), channel_id=1, source_target_pairs={{0,64},{64,0},{128,192},{192,128},{1,65},{65,1},{129,193},{193,129... | collective-permute-start | bytes 49160 | tf_op jit(solution)/shard_map/ppermute | solution.py:354
  130.8 0.6 copy-start.7

commit v3 on v2

--- a/solution.py
+++ b/solution.py
@@ -113,8 +113,8 @@
 
 def terms_kernel(
     side_ref, mine_ref, theirs_ref, mid_ref,
-    midgrad_ref, keep_ref, send_ref,
-    cores, lrows, pick, diag, mix_hi, mix_lo, fterm, lterm, midm, asub, midf,
+    midkeep_ref, midsend_ref, keep_ref, send_ref,
+    cores, lrows, pick, diag, mix_hi, mix_lo, outer, chosen, asub,
 ):
     side = side_ref[0]
     cores[side] = mine_ref[:, 2 * LANES :]
@@ -127,6 +127,8 @@
     across_f = across.astype(F32)
     pick_first = ones_where(across_f == first)
     pick_last = ones_where(across_f == last)
+    chosen[side] = pick_first
+    chosen[1 - side] = pick_last
     arows = nn(pick_first, cores[0]).astype(BF)
     last_rows = nn(pick_last, cores[1]).astype(BF)
     for q in range(8):
@@ -147,18 +149,16 @@
         )
     own = ones_where(iota((SLOTS, 2 * LANES), 0) % GROUP == iota((SLOTS, 2 * LANES), 1) % GROUP)
 
-    def spread(ab, carry):
-        pair = jnp.concatenate([pick[2 * ab], pick[2 * ab + 1]], axis=1)
-        value = nn(grads, pair).astype(BF) * own
-        diag[0, ab] = value[:, 0:LANES]
-        diag[1, ab] = value[:, LANES:]
+    def spread(step, carry):
+        for part in range(8):
+            ab = step * 8 + part
+            pair = jnp.concatenate([pick[2 * ab], pick[2 * ab + 1]], axis=1)
+            value = nn(grads, pair).astype(BF) * own
+            diag[0, ab] = value[:, 0:LANES]
+            diag[1, ab] = value[:, LANES:]
         return carry
 
-    lax.fori_loop(0, D1 * D2, spread, 0)
-
-    for m in range(4):
-        for b in range(D2):
-            midm[m, b] = mid_ref[pl.ds(b * 4 + m, R, stride=4 * D2), :].astype(BF)
+    lax.fori_loop(0, D1 * D2 // 8, spread, 0)
 
     def group(q, carry):
         here = pl.ds(pl.multiple_of(q * GROUP, GROUP), GROUP)
@@ -168,7 +168,7 @@
         total = None
         for b in range(D2):
             head = lax.dot_general(
-                midm[m, b], left, (((0,), (1,)), ((), ())), preferred_element_type=F32
+                mid_ref[m, b], left, (((0,), (1,)), ((), ())), preferred_element_type=F32
             ).astype(BF)
             block = jnp.concatenate(
                 [
@@ -185,59 +185,52 @@
             mix_lo[b, there, :] = lo
         total = total.T
         for c in range(D3):
-            lterm[c, here, :] = total[c * GROUP : (c + 1) * GROUP, :]
+            outer[1 - side, c, here, :] = total[c * GROUP : (c + 1) * GROUP, :]
         return carry
 
     lax.fori_loop(0, 8, group, 0)
 
-    for m in range(4):
-        span = slice(m * SLOTS, (m + 1) * SLOTS)
+    for n in range(4):
+        half = side if n < 2 else 1 - side
+        m = half * 2 + n % 2
+        grad_ref = midkeep_ref if n < 2 else midsend_ref
+        span = pl.ds(pl.multiple_of(m * SLOTS, SLOTS), SLOTS)
         left = jnp.concatenate([asub[2 * m], asub[2 * m + 1]], axis=0)
         part = None
         for b in range(0, D2, 2):
             hi = jnp.concatenate([mix_hi[b, span, :], mix_hi[b + 1, span, :]], axis=1)
             lo = jnp.concatenate([mix_lo[b, span, :], mix_lo[b + 1, span, :]], axis=1)
-            pair = jnp.concatenate([midm[m, b], midm[m, b + 1]], axis=1)
+            pair = jnp.concatenate([mid_ref[m, b], mid_ref[m, b + 1]], axis=1)
             term = nt(jnp.concatenate([hi, lo], axis=1), jnp.concatenate([pair, pair], axis=1))
             part = term if part is None else part + term
-            grad = tn(left, hi) + tn(left, lo)
-            midf[pl.ds(b * 4 + m, R, stride=4 * D2), :] = grad[:, 0:LANES]
-            midf[pl.ds((b + 1) * 4 + m, R, stride=4 * D2), :] = grad[:, LANES:]
+            grad = tn(left, hi)
+            grad_ref[n % 2, b] = grad[:, 0:LANES]
+            grad_ref[n % 2, b + 1] = grad[:, LANES:]
         for q in range(2):
             for a in range(D1):
-                fterm[a, (2 * m + q) * GROUP : (2 * m + q + 1) * GROUP, :] = part[
-                    (q * D1 + a) * GROUP : (q * D1 + a + 1) * GROUP, :
-                ]
-    midgrad_ref[...] = midf[...].astype(BF)
-
-    hi, lo = split_two(jnp.concatenate([fterm[a] for a in range(D1)], axis=1))
-    first_part = tn(pick_first, hi) + tn(pick_first, lo)
-    hi, lo = split_two(jnp.concatenate([lterm[c] for c in range(D3)], axis=1))
-    last_part = tn(pick_last, hi) + tn(pick_last, lo)
-
-    @pl.when(side == 0)
-    def _():
-        keep_ref[...] = first_part
-        send_ref[...] = last_part
-
-    @pl.when(side != 0)
-    def _():
-        keep_ref[...] = last_part
-        send_ref[...] = first_part
+                here = pl.ds(pl.multiple_of((2 * m + q) * GROUP, GROUP), GROUP)
+                outer[side, a, here, :] = part[(q * D1 + a) * GROUP : (q * D1 + a + 1) * GROUP, :]
+
+    for n, ref in ((1, send_ref), (0, keep_ref)):
+        for a in range(0, D1, 2):
+            hi, lo = split_two(jnp.concatenate([outer[n, a], outer[n, a + 1]], axis=1))
+            ref[:, a * LANES : (a + 2) * LANES] = tn(chosen[n], hi) + tn(chosen[n], lo)
 
 
 def terms(side, mine, theirs, mid):
     vmem = pl.BlockSpec(memory_space=pltpu.VMEM)
     width = D1 * R
+    half = (2, D2, R, LANES)
     return pl.pallas_call(
         terms_kernel,
         out_shape=(
-            jax.ShapeDtypeStruct(mid.shape, BF),
+            jax.ShapeDtypeStruct(half, F32),
+            jax.ShapeDtypeStruct(half, F32),
             jax.ShapeDtypeStruct((SLOTS, width), F32),
             jax.ShapeDtypeStruct((SLOTS, width), F32),
         ),
         in_specs=[pl.BlockSpec(memory_space=pltpu.SMEM)] + [vmem] * 3,
-        out_specs=(vmem, vmem, vmem),
+        out_specs=(vmem,) * 4,
         scratch_shapes=[
             pltpu.VMEM((2, SLOTS, width), BF),
             pltpu.VMEM((8, D3 * GROUP, LANES), BF),
@@ -245,20 +238,74 @@
             pltpu.VMEM((2, D1 * D2, SLOTS, LANES), BF),
             pltpu.VMEM((D2, 4 * SLOTS, LANES), BF),
             pltpu.VMEM((D2, 4 * SLOTS, LANES), BF),
-            pltpu.VMEM((D1, SLOTS, LANES), F32),
-            pltpu.VMEM((D3, SLOTS, LANES), F32),
-            pltpu.VMEM((4, D2, R, LANES), BF),
+            pltpu.VMEM((2, D1, SLOTS, LANES), F32),
+            pltpu.VMEM((2, SLOTS, SLOTS), BF),
             pltpu.VMEM((8, D1 * GROUP, R), BF),
-            pltpu.VMEM(mid.shape, F32),
         ],
         interpret=INTERPRET,
         name="terms",
     )(side, mine, theirs, mid)
 
 
-def outer_kernel(side_ref, mine_ref, theirs_ref, *refs):
+R_BLOCK = 16
+
+
+def mid_copy_kernel(core_ref, out_ref):
+    for m in range(4):
+        for b in range(D2):
+            out_ref[m, b] = core_ref[pl.ds(b * 4 + m, R_BLOCK, stride=4 * D2), :].astype(BF)
+
+
+def mid_round(core):
+    return pl.pallas_call(
+        mid_copy_kernel,
+        grid=(R // R_BLOCK,),
+        out_shape=jax.ShapeDtypeStruct((4, D2, R, LANES), BF),
+        in_specs=[pl.BlockSpec((R_BLOCK * D2 * 4, LANES), lambda i: (i, 0))],
+        out_specs=pl.BlockSpec((4, D2, R_BLOCK, LANES), lambda i: (0, 0, i, 0)),
+        interpret=INTERPRET,
+        name="mid_round",
+    )(core)
+
+
+def mid_kernel(
+    side_ref, core_ref, moment_ref, second_ref, near_ref, far_ref, near_rest_ref, far_rest_ref,
+    core_out, moment_out, second_out, grad,
+):
     side = side_ref[0]
-    mine, theirs = mine_ref[...], theirs_ref[...]
+    for i in range(2):
+        for b in range(D2):
+            own = near_ref[i, b].astype(F32) + far_ref[i, b].astype(F32)
+            rest = near_rest_ref[i, b].astype(F32) + far_rest_ref[i, b].astype(F32)
+            at = b * 4 + i
+            grad[pl.ds(at + side * 2, R_BLOCK, stride=4 * D2), :] = own
+            grad[pl.ds(at + (1 - side) * 2, R_BLOCK, stride=4 * D2), :] = rest
+    core, moment, second = adam_update(core_ref[...], moment_ref[...], second_ref[...], grad[...])
+    core_out[...] = core
+    moment_out[...] = moment
+    second_out[...] = second
+
+
+def mid_step(side, states, parts):
+    rows = R_BLOCK * D2 * 4
+    state = pl.BlockSpec((rows, LANES), lambda i: (i, 0))
+    part = pl.BlockSpec((2, D2, R_BLOCK, LANES), lambda i: (0, 0, i, 0))
+    return pl.pallas_call(
+        mid_kernel,
+        grid=(R // R_BLOCK,),
+        out_shape=tuple(jax.ShapeDtypeStruct(states[0].shape, F32) for _ in range(3)),
+        in_specs=[pl.BlockSpec(memory_space=pltpu.SMEM)] + [state] * 3 + [part] * 4,
+        out_specs=(state,) * 3,
+        scratch_shapes=[pltpu.VMEM((rows, LANES), F32)],
+        interpret=INTERPRET,
+        name="mid_step",
+    )(side, *states, *parts)
+
+
+def outer_kernel(side_ref, own_ref, chip_ref, core_ref, both_ref, *refs):
+    side = side_ref[0]
+    mine = own_ref[...] + chip_ref[...]
+    theirs = core_ref[...] + both_ref[...]
     first_grad = jnp.where(side == 0, mine, theirs)
     last_grad = jnp.where(side == 0, theirs, mine)
     width = mine.shape[1]
@@ -275,16 +322,17 @@
         ref[...] = value
 
 
-def outer_step(side, mine, theirs, states):
+def outer_step(side, shares, states):
     vmem = pl.BlockSpec(memory_space=pltpu.VMEM)
+    mine = shares[0]
     return pl.pallas_call(
         outer_kernel,
         out_shape=tuple(jax.ShapeDtypeStruct(mine.shape, F32) for _ in range(6)),
-        in_specs=[pl.BlockSpec(memory_space=pltpu.SMEM)] + [vmem] * 8,
+        in_specs=[pl.BlockSpec(memory_space=pltpu.SMEM)] + [vmem] * 10,
         out_specs=(vmem,) * 6,
         interpret=INTERPRET,
         name="outer",
-    )(side, mine, theirs, *states)
+    )(side, *shares, *states)
 
 
 def row_tiles(x):
@@ -297,6 +345,7 @@
 
 CORE_SWAP = ((0, 1), (1, 0), (2, 3), (3, 2))
 CHIP_SWAP = ((0, 2), (2, 0), (1, 3), (3, 1))
+BOTH_SWAP = ((0, 3), (3, 0), (1, 2), (2, 1))
 
 
 def local(
@@ -326,36 +375,35 @@
         first_core,
         last_core,
     )
+    mid_rows = row_tiles(mid_core)
     mine = lax.all_to_all(packed, "dp", split_axis=0, concat_axis=0, tiled=True)
+    mid_copy = mid_round(mid_rows)
     theirs = lax.ppermute(mine, "rep", CORE_SWAP)
-    mid_part, keep, send = terms(side, mine, theirs, row_tiles(mid_core))
-
-    mid_other = lax.ppermute(mid_part, "rep", CORE_SWAP)
+    mid_keep, mid_send, keep, send = terms(side, mine, theirs, mid_copy)
+
+    mid_other = lax.ppermute(mid_send, "rep", CORE_SWAP)
     other = lax.ppermute(send, "rep", CORE_SWAP)
-    half_rows = mid_part.shape[0] // 2
-    mid_chip = (mid_part.astype(F32) + mid_other.astype(F32)).astype(BF)
-    half = lax.dynamic_slice_in_dim(mid_chip, side[0] * half_rows, half_rows, axis=0)
-    half, chip_sum = lax.optimization_barrier((half, (keep + other).astype(BF)))
-    far_half = lax.ppermute(half, "rep", CHIP_SWAP)
+    near = (mid_keep + mid_other).astype(BF)
+    near, chip_sum = lax.optimization_barrier((near, (keep + other).astype(BF)))
+    far = lax.ppermute(near, "rep", CHIP_SWAP)
     share = lax.all_to_all(chip_sum, "dp", split_axis=0, concat_axis=0, tiled=True)
-    far_rest = lax.ppermute(far_half, "rep", CORE_SWAP)
-    far = jnp.where(
-        side[0] == 0,
-        jnp.concatenate([far_half, far_rest], axis=0),
-        jnp.concatenate([far_rest, far_half], axis=0),
+    near_rest = lax.ppermute(near, "rep", CORE_SWAP)
+    far_rest = lax.ppermute(far, "rep", CORE_SWAP)
+    mid_next = mid_step(
+        side,
+        (mid_rows, row_tiles(mid_moment), row_tiles(mid_second)),
+        (near, far, near_rest, far_rest),
     )
-    mid_grad = mid_chip.astype(F32) + far.astype(F32)
-    mid_next = adam_update(row_tiles(mid_core), row_tiles(mid_moment), row_tiles(mid_second), mid_grad)
+
     share, *mid_next = lax.optimization_barrier((share, *mid_next))
     mid_next = tuple(untile(x) for x in mid_next)
     share = jnp.sum(share.reshape(N_SRC, -1, share.shape[1]).astype(F32), axis=0)
-
-    share = share + lax.ppermute(share, "rep", CHIP_SWAP)
-    other_share = lax.ppermute(share, "rep", CORE_SWAP)
+    swapped = tuple(
+        lax.ppermute(share, "rep", pairs) for pairs in (CHIP_SWAP, CORE_SWAP, BOTH_SWAP)
+    )
     outer = outer_step(
         side,
-        share,
-        other_share,
+        (share,) + swapped,
         (first_core, first_moment, first_second, last_core, last_moment, last_second),
     )
     return outer[:3] + mid_next + outer[3:]

time: 134 us -> 114 us (0.85)
  waiting for transfers between devices: 29.2 us -> 13.5 us
  other arithmetic: 13.8 us -> 2.41 us
  Pallas kernels: 34.9 us -> 41.6 us
    all_to_all x1, waiting for transfers between devices: 11.2 us -> 0.01 us  [local(): lax.all_to_all(chip_sum, 'dp', split_axis=0, concat_axis=0, tiled=True)]
    pallas_call x1 -> x3, Pallas kernels: 30.7 us -> 37.4 us  [the longest x1 22.6 us: terms(): pl.pallas_call(terms_kernel, out_shape=(jax.ShapeDtypeStruct(half, F32),...]
    sub x1 -> x0, other arithmetic: 6.45 us -> none  [adam_update(): current - LEARN_RATE * corrected / (spread + EPSILON)]
    mul x2 -> x0, other arithmetic: 3.72 us -> none  [the longest x1 1.86 us: adam_update(): second_next = BETA_TWO * second + (1.0 - BETA_TWO) * gradient * gradient]
    ppermute x5 -> x7, waiting for transfers between devices: 16 us -> 13.4 us  [the longest x1 8.08 us: local(): far = lax.ppermute(near, 'rep', CHIP_SWAP)]
    ppermute x1, waiting for transfers between devices: 1.91 us -> 0.01 us  [local(): theirs = lax.ppermute(mine, 'rep', CORE_SWAP)]
    unnamed x16 -> x22, local copies, waits for them, and re-layouts: 1.89 us -> 2.9 us
    ppermute x5 -> x7, starting transfers between devices: 5.99 us -> 5 us  [the longest x3 1.95 us: local(): lax.ppermute(share, 'rep', pairs)]
  transfers between devices with their start and end apart: 8 -> 10, of which waited for: 6 -> 5; matrix products, arithmetic and copies ran while one was open for 9% -> 1% of each run, Pallas kernels for 0% -> 13%
where the time goes in v3:
time: 114 us; the launch traced here: 113 us
  Pallas kernels  41.6 us (36%)
  blocking collectives  37.6 us (33%)
  starting transfers between devices  14.5 us (13%)
  waiting for transfers between devices  13.5 us (12%)
  local copies, waits for them, and re-layouts  2.9 us (3%)
  other arithmetic  2.41 us (2%)
    all_to_all x1, blocking collectives, local(): mine = lax.all_to_all(packed, 'dp', split_axis=0, concat_axis=0, tiled=True)  37.6 us
    pallas_call x1, Pallas kernels, terms(): pl.pallas_call(terms_kernel, out_shape=(jax.ShapeDtypeStruct(half, F32),...  22.6 us
    pallas_call x1, Pallas kernels, mid_step(): pl.pallas_call(mid_kernel, grid=(R // R_BLOCK,), out_shape=tuple((jax.Sha...  8.9 us
    ppermute x1, waiting for transfers between devices, local(): far = lax.ppermute(near, 'rep', CHIP_SWAP)  8.08 us
    all_to_all x1, starting transfers between devices, local(): lax.all_to_all(chip_sum, 'dp', split_axis=0, concat_axis=0, tiled=True)  6.31 us
    pallas_call x1, Pallas kernels, mid_round(): pl.pallas_call(mid_copy_kernel, grid=(R // R_BLOCK,), out_shape=jax.Shape...  5.89 us
    unnamed x22, local copies, waits for them, and re-layouts  2.9 us
    ppermute x1, starting transfers between devices, local(): theirs = lax.ppermute(mine, 'rep', CORE_SWAP)  2.88 us
  transfers between devices with their start and end apart: 10, of which 5 were waited for; matrix products, arithmetic and copies ran while one was open for 1% of the time, Pallas kernels for 13%

profile of v3, /device:TPU:1, one launch (start us, length us, event | category | flops | bytes accessed | tf_op | source)
XLA Modules:
  0.0 113.3 jit_solution(123130019278801989)
XLA Ops:
  0.7 2.4 %pack.1 = bf16[512,768]{1,0:T(8,128)(2,1)} custom-call(s32[1]{0:T(128)} %bitcast.side_ref, s32[1,256]{1,0:T(1,128)} %bitcast.49, s32[1,256]{1,0:T(1,128)} %bitcast.50, s32[1,256]{1,0:T(1,128)} %bitcast.51, s32[1,16]{1,0:T(1,128)} %bag_ref.1, bf16[16,128]{1,0:T(8,128)(2,1)} %cot_ref.1, f32[8,512]{1,0:T(8,128)} %refs_0_.1, f32[8,512]{1,0:T(8,128)} %refs_3_.1), custom_call_target="tpu_custom_call" | custom-call | tf_op jit(solution)/shard_map/pack/pallas_call | solution.py:104
  3.0 37.6 %all_to_all.23 = bf16[64,8,768]{2,1,0:T(8,128)(2,1)S(1)} all-to-all(bf16[64,8,768]{2,1,0:T(8,128)(2,1)} %bitcast.43), channel_id=1, replica_groups=mesh['rep'=4,'dp'=64] {'dp'}, dimensions={0} | all-to-all | bytes 1572864 | tf_op jit(solution)/shard_map/all_to_all | solution.py:379
  40.7 2.9 %collective-permute-start = (bf16[512,768]{1,0:T(8,128)(2,1)S(1)}, bf16[512,768]{1,0:T(8,128)(2,1)S(1)}, u32[]{:S(2)}, u32[]{:S(2)}) collective-permute-start(bf16[512,768]{1,0:T(8,128)(2,1)S(1)} %bitcast.44), channel_id=1, source_target_pairs={{0,64},{64,0},{128,192},{192,128},{1,65},{65,1},{129,193},{193,129... | collective-permute-start | bytes 2359304 | tf_op jit(solution)/shard_map/ppermute | solution.py:381
  43.5 5.9 %mid_round.1.mid_ref = bf16[4,8,128,128]{3,2,1,0:T(8,128)(2,1)} custom-call(f32[4096,128]{1,0:T(8,128)} %bitcast.41), custom_call_target="tpu_custom_call" | custom-call | tf_op jit(solution)/shard_map/mid_round/pallas_call | solution.py:260
  49.4 0.9 copy-done.3
  50.3 22.6 %terms.1 = (f32[2,8,128,128]{3,2,1,0:T(8,128)}, f32[2,8,128,128]{3,2,1,0:T(8,128)}, f32[512,512]{1,0:T(8,128)}, f32[512,512]{1,0:T(8,128)}) custom-call(s32[1]{0:T(128)} %bitcast.side_ref, bf16[512,768]{1,0:T(8,128)(2,1)} %bitcast.45, bf16[512,768]{1,0:T(8,128)(2,1)} %copy-done.3, bf16[4,8,128,128]{3,2,1,0:T(8,128)(2,1)} %mid_round.1.mid_ref), custom_call_target="tpu_custom_call" | custom-call | tf_op jit(solution)/shard_map/terms/pallas_call | solution.py:224
  73.2 0.3 collective-permute-start.2
  73.5 2.4 %collective-permute-done.1 = f32[2,8,128,128]{3,2,1,0:T(8,128)S(1)} collective-permute-done((f32[2,8,128,128]{3,2,1,0:T(8,128)}, f32[2,8,128,128]{3,2,1,0:T(8,128)S(1)}, u32[]{:S(2)}, u32[]{:S(2)}) %collective-permute-start.1) | collective-permute-done | bytes 1048608 | tf_op jit(solution)/shard_map/ppermute | solution.py:384
  75.8 1.3 %add_convert_fusion.1.near_ref = bf16[2,8,128,128]{3,2,1,0:T(8,128)(2,1)S(1)} fusion(f32[2,8,128,128]{3,2,1,0:T(8,128)} %get-tuple-element.28, f32[2,8,128,128]{3,2,1,0:T(8,128)S(1)} %collective-permute-done.1), kind=kLoop, calls=%fused_computation.2 | loop fusion | flops 524288 | bytes 2621440 | tf_op jit(solution)/shard_map/convert_element_type | solution.py:386
  77.3 1.0 add_convert_fusion
  78.3 0.4 collective-permute-start.3
  78.7 6.3 %all-to-all-start.1 = ((bf16[64,8,512]{2,1,0:T(8,128)(2,1)}), bf16[64,8,512]{2,1,0:T(8,128)(2,1)S(1)}, u32[]{:S(2)}, u32[]{:S(2)}) async-start(bf16[64,8,512]{2,1,0:T(8,128)(2,1)} %bitcast.9), calls=%async_computation.1 | async-start | bytes 1048576 | tf_op jit(solution)/shard_map/all_to_all | solution.py:389
  85.0 0.9 collective-permute-start.4
  85.9 8.1 %collective-permute-done.3.far_ref = bf16[2,8,128,128]{3,2,1,0:T(8,128)(2,1)S(1)} collective-permute-done((bf16[2,8,128,128]{3,2,1,0:T(8,128)(2,1)S(1)}, bf16[2,8,128,128]{3,2,1,0:T(8,128)(2,1)S(1)}, u32[]{:S(2)}, u32[]{:S(2)}) %collective-permute-start.3) | collective-permute-done | bytes 524320 | tf_op jit(solution)/shard_map/ppermute | solution.py:388
  94.0 1.6 %collective-permute-start.5 = (bf16[2,8,128,128]{3,2,1,0:T(8,128)(2,1)S(1)}, bf16[2,8,128,128]{3,2,1,0:T(8,128)(2,1)S(1)}, u32[]{:S(2)}, u32[]{:S(2)}) collective-permute-start(bf16[2,8,128,128]{3,2,1,0:T(8,128)(2,1)S(1)} %collective-permute-done.3.far_ref), channel_id=1, source_target_pairs={{0,64},{64,0},{128,192},{192,128},{1,65},{65,1},{129,193},{193,129... | collective-permute-start | bytes 1572872 | tf_op jit(solution)/shard_map/ppermute | solution.py:391
  95.6 1.5 %collective-permute-done.5.far_rest_ref = bf16[2,8,128,128]{3,2,1,0:T(8,128)(2,1)S(1)} collective-permute-done((bf16[2,8,128,128]{3,2,1,0:T(8,128)(2,1)S(1)}, bf16[2,8,128,128]{3,2,1,0:T(8,128)(2,1)S(1)}, u32[]{:S(2)}, u32[]{:S(2)}) %collective-permute-start.5) | collective-permute-done | bytes 524320 | tf_op jit(solution)/shard_map/ppermute | solution.py:391
  97.1 0.8 copy-done.6
  97.9 8.9 %mid_step.1 = (f32[4096,128]{1,0:T(8,128)}, f32[4096,128]{1,0:T(8,128)}, f32[4096,128]{1,0:T(8,128)}) custom-call(s32[1]{0:T(128)} %bitcast.side_ref, f32[4096,128]{1,0:T(8,128)} %bitcast.42, f32[4096,128]{1,0:T(8,128)} %bitcast.47, f32[4096,128]{1,0:T(8,128)} %bitcast.48, bf16[2,8,128,128]{3,2,1,0:T(8,128)(2,1)} %copy-done.1, ...), custom_call_target="tpu_custom_call" | custom-call | tf_op jit(solution)/shard_map/mid_step/pallas_call | solution.py:293
  106.9 0.3 collective-permute-start.8
  107.5 1.4 %collective-permute-start.6 = (f32[8,512]{1,0:T(8,128)S(1)}, f32[8,512]{1,0:T(8,128)S(1)}, u32[]{:S(2)}, u32[]{:S(2)}) collective-permute-start(f32[8,512]{1,0:T(8,128)S(1)} %convert_reduce_fusion.own_ref), channel_id=1, source_target_pairs={{0,128},{128,0},{64,192},{192,64},{1,129},{129,1},{65,193},{193,65... | collective-permute-start | bytes 49160 | tf_op jit(solution)/shard_map/ppermute | solution.py:402
  108.9 1.4 %collective-permute-done.8.both_ref = f32[8,512]{1,0:T(8,128)S(1)} collective-permute-done((f32[8,512]{1,0:T(8,128)S(1)}, f32[8,512]{1,0:T(8,128)S(1)}, u32[]{:S(2)}, u32[]{:S(2)}) %collective-permute-start.8) | collective-permute-done | bytes 16416 | tf_op jit(solution)/shard_map/ppermute | solution.py:402
  110.3 0.6 copy-done.8
  110.9 0.6 copy-done.10
  111.5 1.8 %outer.1 = (f32[8,512]{1,0:T(8,128)}, f32[8,512]{1,0:T(8,128)}, f32[8,512]{1,0:T(8,128)}, f32[8,512]{1,0:T(8,128)}, f32[8,512]{1,0:T(8,128)}, /*index=5*/f32[8,512]{1,0:T(8,128)}) custom-call(s32[1]{0:T(128)} %bitcast.side_ref, f32[8,512]{1,0:T(8,128)} %copy-done.7, f32[8,512]{1,0:T(8,128)} %copy-done.10, f32[8,512]{1,0:T(8,128)} %copy-done.9, ...), custom_call_target="tpu_custom_call" | custom-call | tf_op jit(solution)/shard_map/outer/pallas_call | solution.py:328
  (27 shorter events, 0.7 us)
Async XLA Ops:
  40.7 8.8 %copy-start = (bf16[64,8,768]{2,1,0:T(8,128)(2,1)}, bf16[64,8,768]{2,1,0:T(8,128)(2,1)S(1)}, u32[]{:S(2)}) copy-start(bf16[64,8,768]{2,1,0:T(8,128)(2,1)S(1)} %all_to_all.23) | copy-start | bytes 2359300
  40.7 8.8 %collective-permute-start = (bf16[512,768]{1,0:T(8,128)(2,1)S(1)}, bf16[512,768]{1,0:T(8,128)(2,1)S(1)}, u32[]{:S(2)}, u32[]{:S(2)}) collective-permute-start(bf16[512,768]{1,0:T(8,128)(2,1)S(1)} %bitcast.44), channel_id=1, source_target_pairs={{0,64},{64,0},{128,192},{192,128},{1,65},{65,1},{129,193},{193,129... | collective-permute-start | bytes 2359304 | tf_op jit(solution)/shard_map/ppermute | solution.py:381
  49.4 0.9 copy-start.3
  73.0 4.4 %copy-start.2 = (f32[512,512]{1,0:T(8,128)S(1)}, f32[512,512]{1,0:T(8,128)}, u32[]{:S(2)}) copy-start(f32[512,512]{1,0:T(8,128)} %get-tuple-element.30) | copy-start | bytes 3145732
  73.0 2.9 %collective-permute-start.1 = (f32[2,8,128,128]{3,2,1,0:T(8,128)}, f32[2,8,128,128]{3,2,1,0:T(8,128)S(1)}, u32[]{:S(2)}, u32[]{:S(2)}) collective-permute-start(f32[2,8,128,128]{3,2,1,0:T(8,128)} %get-tuple-element.29), channel_id=1, source_target_pairs={{0,64},{64,0},{128,192},{192,128},{1,65},{65,1},{129,193},{193,129... | collective-permute-start | bytes 3145736 | tf_op jit(solution)/shard_map/ppermute | solution.py:384
  73.2 4.2 %collective-permute-start.2 = (f32[512,512]{1,0:T(8,128)}, f32[512,512]{1,0:T(8,128)S(1)}, u32[]{:S(2)}, u32[]{:S(2)}) collective-permute-start(f32[512,512]{1,0:T(8,128)} %get-tuple-element.31), channel_id=1, source_target_pairs={{0,64},{64,0},{128,192},{192,128},{1,65},{65,1},{129,193},{193,129... | collective-permute-start | bytes 3145736 | tf_op jit(solution)/shard_map/ppermute | solution.py:385
  77.2 19.9 %copy-start.1 = (bf16[2,8,128,128]{3,2,1,0:T(8,128)(2,1)}, bf16[2,8,128,128]{3,2,1,0:T(8,128)(2,1)S(1)}, u32[]{:S(2)}) copy-start(bf16[2,8,128,128]{3,2,1,0:T(8,128)(2,1)S(1)} %add_convert_fusion.1.near_ref) | copy-start | bytes 1572868
  78.3 15.7 %collective-permute-start.3 = (bf16[2,8,128,128]{3,2,1,0:T(8,128)(2,1)S(1)}, bf16[2,8,128,128]{3,2,1,0:T(8,128)(2,1)S(1)}, u32[]{:S(2)}, u32[]{:S(2)}) collective-permute-start(bf16[2,8,128,128]{3,2,1,0:T(8,128)(2,1)S(1)} %add_convert_fusion.1.near_ref), channel_id=1, source_target_pairs={{0,128},{128,0},{64,192},{192,64},{1,129},{129,1},{65,193},{193,65... | collective-permute-start | bytes 1572872 | tf_op jit(solution)/shard_map/ppermute | solution.py:388
  78.7 28.1 %all-to-all-start.1 = ((bf16[64,8,512]{2,1,0:T(8,128)(2,1)}), bf16[64,8,512]{2,1,0:T(8,128)(2,1)S(1)}, u32[]{:S(2)}, u32[]{:S(2)}) async-start(bf16[64,8,512]{2,1,0:T(8,128)(2,1)} %bitcast.9), calls=%async_computation.1 | async-start | bytes 1048576 | tf_op jit(solution)/shard_map/all_to_all | solution.py:389
  85.0 10.6 %collective-permute-start.4 = (bf16[2,8,128,128]{3,2,1,0:T(8,128)(2,1)S(1)}, bf16[2,8,128,128]{3,2,1,0:T(8,128)(2,1)S(1)}, u32[]{:S(2)}, u32[]{:S(2)}) collective-permute-start(bf16[2,8,128,128]{3,2,1,0:T(8,128)(2,1)S(1)} %add_convert_fusion.1.near_ref), channel_id=1, source_target_pairs={{0,64},{64,0},{128,192},{192,128},{1,65},{65,1},{129,193},{193,129... | collective-permute-start | bytes 1572872 | tf_op jit(solution)/shard_map/ppermute | solution.py:390
  94.0 3.2 %copy-start.4 = (bf16[2,8,128,128]{3,2,1,0:T(8,128)(2,1)}, bf16[2,8,128,128]{3,2,1,0:T(8,128)(2,1)S(1)}, u32[]{:S(2)}) copy-start(bf16[2,8,128,128]{3,2,1,0:T(8,128)(2,1)S(1)} %collective-permute-done.3.far_ref) | copy-start | bytes 1572868
  94.0 3.2 %collective-permute-start.5 = (bf16[2,8,128,128]{3,2,1,0:T(8,128)(2,1)S(1)}, bf16[2,8,128,128]{3,2,1,0:T(8,128)(2,1)S(1)}, u32[]{:S(2)}, u32[]{:S(2)}) collective-permute-start(bf16[2,8,128,128]{3,2,1,0:T(8,128)(2,1)S(1)} %collective-permute-done.3.far_ref), channel_id=1, source_target_pairs={{0,64},{64,0},{128,192},{192,128},{1,65},{65,1},{129,193},{193,129... | collective-permute-start | bytes 1572872 | tf_op jit(solution)/shard_map/ppermute | solution.py:391
  95.6 1.5 %copy-start.5 = (bf16[2,8,128,128]{3,2,1,0:T(8,128)(2,1)}, bf16[2,8,128,128]{3,2,1,0:T(8,128)(2,1)S(1)}, u32[]{:S(2)}) copy-start(bf16[2,8,128,128]{3,2,1,0:T(8,128)(2,1)S(1)} %collective-permute-done.4.near_rest_ref) | copy-start | bytes 1572868
  97.1 0.8 copy-start.6
  106.9 3.3 %copy-start.7 = (f32[8,512]{1,0:T(8,128)}, f32[8,512]{1,0:T(8,128)S(1)}, u32[]{:S(2)}) copy-start(f32[8,512]{1,0:T(8,128)S(1)} %convert_reduce_fusion.own_ref) | copy-start | bytes 49156
  106.9 3.3 %collective-permute-start.8 = (f32[8,512]{1,0:T(8,128)S(1)}, f32[8,512]{1,0:T(8,128)S(1)}, u32[]{:S(2)}, u32[]{:S(2)}) collective-permute-start(f32[8,512]{1,0:T(8,128)S(1)} %convert_reduce_fusion.own_ref), channel_id=1, source_target_pairs={{0,192},{192,0},{64,128},{128,64},{1,193},{193,1},{65,129},{129,65... | collective-permute-start | bytes 49160 | tf_op jit(solution)/shard_map/ppermute | solution.py:402
  107.3 3.0 %collective-permute-start.7 = (f32[8,512]{1,0:T(8,128)S(1)}, f32[8,512]{1,0:T(8,128)S(1)}, u32[]{:S(2)}, u32[]{:S(2)}) collective-permute-start(f32[8,512]{1,0:T(8,128)S(1)} %convert_reduce_fusion.own_ref), channel_id=1, source_target_pairs={{0,64},{64,0},{128,192},{192,128},{1,65},{65,1},{129,193},{193,129... | collective-permute-start | bytes 49160 | tf_op jit(solution)/shard_map/ppermute | solution.py:402
  107.5 2.8 %collective-permute-start.6 = (f32[8,512]{1,0:T(8,128)S(1)}, f32[8,512]{1,0:T(8,128)S(1)}, u32[]{:S(2)}, u32[]{:S(2)}) collective-permute-start(f32[8,512]{1,0:T(8,128)S(1)} %convert_reduce_fusion.own_ref), channel_id=1, source_target_pairs={{0,128},{128,0},{64,192},{192,64},{1,129},{129,1},{65,193},{193,65... | collective-permute-start | bytes 49160 | tf_op jit(solution)/shard_map/ppermute | solution.py:402
  110.3 0.6 copy-start.8
  110.3 0.6 copy-start.9
  110.9 0.6 copy-start.10

commit v4 on v3

--- a/solution.py
+++ b/solution.py
@@ -15,7 +15,8 @@
 LANES = 128
 N_SRC = 64
 SLOTS = 512
-GROUP = 64
+GROUP = 32
+GROUPS = 16
 
 LEARN_RATE = 0.01
 BETA_ONE = 0.9
@@ -30,9 +31,9 @@
 def adam_update(current, moment, second, gradient):
     moment_next = BETA_ONE * moment + (1.0 - BETA_ONE) * gradient
     second_next = BETA_TWO * second + (1.0 - BETA_TWO) * gradient * gradient
-    corrected = moment_next / (1.0 - BETA_ONE**STEP)
-    spread = jnp.sqrt(second_next / (1.0 - BETA_TWO**STEP))
-    return (current - LEARN_RATE * corrected / (spread + EPSILON), moment_next, second_next)
+    corrected = moment_next * (LEARN_RATE / (1.0 - BETA_ONE**STEP))
+    spread = jnp.sqrt(second_next * (1.0 / (1.0 - BETA_TWO**STEP)))
+    return (current - corrected / (spread + EPSILON), moment_next, second_next)
 
 
 def iota(shape, axis):
@@ -120,7 +121,8 @@
     cores[side] = mine_ref[:, 2 * LANES :]
     cores[1 - side] = theirs_ref[:, 2 * LANES :]
     up, across = iota((SLOTS, SLOTS), 0), iota((SLOTS, SLOTS), 1)
-    slots = nn(ones_where(across == (up % GROUP) * 8 + up // GROUP), mine_ref[:, 0 : 2 * LANES])
+    source = (up // GROUP % 2) * GROUP + up % GROUP
+    slots = nn(ones_where(across == source * 8 + up // (2 * GROUP)), mine_ref[:, 0 : 2 * LANES])
     grads = slots[:, 0:LANES].astype(BF)
     first = slots[:, LANES : LANES + 1] * 32.0 + slots[:, LANES + 1 : LANES + 2]
     last = slots[:, LANES + 2 : LANES + 3] * 32.0 + slots[:, LANES + 3 : LANES + 4]
@@ -131,7 +133,7 @@
     chosen[1 - side] = pick_last
     arows = nn(pick_first, cores[0]).astype(BF)
     last_rows = nn(pick_last, cores[1]).astype(BF)
-    for q in range(8):
+    for q in range(GROUPS):
         for c in range(D3):
             lrows[q, c * GROUP : (c + 1) * GROUP, :] = last_rows[
                 q * GROUP : (q + 1) * GROUP, c * LANES : (c + 1) * LANES
@@ -143,59 +145,62 @@
 
     pick[...] = jnp.zeros(pick.shape, BF)
     tile_row, tile_lane = iota((16, LANES), 0), iota((16, LANES), 1)
-    for i in range(2 * D1 * D2):
-        pick[i, (i // 8) * 16 : (i // 8) * 16 + 16, :] = ones_where(
-            tile_row == 2 * (i % 8) + tile_lane // GROUP
+    for ab in range(D1 * D2):
+        pick[ab, (ab // 4) * 16 : (ab // 4) * 16 + 16, :] = ones_where(
+            tile_row == D3 * (ab % 4) + tile_lane // GROUP
         )
     own = ones_where(iota((SLOTS, 2 * LANES), 0) % GROUP == iota((SLOTS, 2 * LANES), 1) % GROUP)
 
     def spread(step, carry):
-        for part in range(8):
-            ab = step * 8 + part
-            pair = jnp.concatenate([pick[2 * ab], pick[2 * ab + 1]], axis=1)
+        for part in range(4):
+            ab = step * 8 + part * 2
+            pair = jnp.concatenate([pick[ab], pick[ab + 1]], axis=1)
             value = nn(grads, pair).astype(BF) * own
-            diag[0, ab] = value[:, 0:LANES]
-            diag[1, ab] = value[:, LANES:]
+            diag[ab] = value[:, 0:LANES]
+            diag[ab + 1] = value[:, LANES:]
         return carry
 
     lax.fori_loop(0, D1 * D2 // 8, spread, 0)
 
-    def group(q, carry):
-        here = pl.ds(pl.multiple_of(q * GROUP, GROUP), GROUP)
-        m = q // 2
-        left = asub[q]
-        weights = lrows[q]
-        total = None
-        for b in range(D2):
-            head = lax.dot_general(
-                mid_ref[m, b], left, (((0,), (1,)), ((), ())), preferred_element_type=F32
-            ).astype(BF)
-            block = jnp.concatenate(
-                [
-                    jnp.concatenate([diag[h, a * D2 + b, here, :] for a in range(D1)], axis=0)
-                    for h in range(2)
-                ],
-                axis=1,
-            )
-            part = nn(head, block)
-            total = part if total is None else total + part
-            hi, lo = split_two(nn(block, weights))
-            there = pl.ds(pl.multiple_of(q * D1 * GROUP, D1 * GROUP), D1 * GROUP)
-            mix_hi[b, there, :] = hi
-            mix_lo[b, there, :] = lo
-        total = total.T
-        for c in range(D3):
-            outer[1 - side, c, here, :] = total[c * GROUP : (c + 1) * GROUP, :]
+    def row(m, carry):
+        left = jnp.concatenate([asub[4 * m + g] for g in range(4)], axis=0)
+        totals = [None] * 4
+        for b in range(0, D2, 2):
+            heads = [
+                lax.dot_general(
+                    mid_ref[m, b + i], left, (((0,), (1,)), ((), ())), preferred_element_type=F32
+                ).astype(BF)
+                for i in range(2)
+            ]
+            for g in range(4):
+                q = 4 * m + g
+                here = pl.ds(pl.multiple_of(q * GROUP, GROUP), GROUP)
+                there = pl.ds(pl.multiple_of(q * D1 * GROUP, D1 * GROUP), D1 * GROUP)
+                block = jnp.concatenate(
+                    [diag[a * D2 + b + i, here, :] for i in range(2) for a in range(D1)], axis=0
+                )
+                head = jnp.concatenate([h[:, g * LANES : (g + 1) * LANES] for h in heads], axis=1)
+                part = nn(head, block)
+                totals[g] = part if totals[g] is None else totals[g] + part
+                hi, lo = split_two(nn(block, lrows[q]))
+                for i in range(2):
+                    mix_hi[b + i, there, :] = hi[i * LANES : (i + 1) * LANES]
+                    mix_lo[b + i, there, :] = lo[i * LANES : (i + 1) * LANES]
+        for g in range(4):
+            here = pl.ds(pl.multiple_of((4 * m + g) * GROUP, GROUP), GROUP)
+            total = totals[g].T
+            for c in range(D3):
+                outer[1 - side, c, here, :] = total[c * GROUP : (c + 1) * GROUP, :]
         return carry
 
-    lax.fori_loop(0, 8, group, 0)
+    lax.fori_loop(0, 4, row, 0)
 
     for n in range(4):
         half = side if n < 2 else 1 - side
         m = half * 2 + n % 2
         grad_ref = midkeep_ref if n < 2 else midsend_ref
         span = pl.ds(pl.multiple_of(m * SLOTS, SLOTS), SLOTS)
-        left = jnp.concatenate([asub[2 * m], asub[2 * m + 1]], axis=0)
+        left = jnp.concatenate([asub[4 * m + g] for g in range(4)], axis=0)
         part = None
         for b in range(0, D2, 2):
             hi = jnp.concatenate([mix_hi[b, span, :], mix_hi[b + 1, span, :]], axis=1)
@@ -206,9 +211,9 @@
             grad = tn(left, hi)
             grad_ref[n % 2, b] = grad[:, 0:LANES]
             grad_ref[n % 2, b + 1] = grad[:, LANES:]
-        for q in range(2):
+        for q in range(4):
             for a in range(D1):
-                here = pl.ds(pl.multiple_of((2 * m + q) * GROUP, GROUP), GROUP)
+                here = pl.ds(pl.multiple_of((4 * m + q) * GROUP, GROUP), GROUP)
                 outer[side, a, here, :] = part[(q * D1 + a) * GROUP : (q * D1 + a + 1) * GROUP, :]
 
     for n, ref in ((1, send_ref), (0, keep_ref)):
@@ -233,14 +238,14 @@
         out_specs=(vmem,) * 4,
         scratch_shapes=[
             pltpu.VMEM((2, SLOTS, width), BF),
-            pltpu.VMEM((8, D3 * GROUP, LANES), BF),
-            pltpu.VMEM((2 * D1 * D2, LANES, LANES), BF),
-            pltpu.VMEM((2, D1 * D2, SLOTS, LANES), BF),
+            pltpu.VMEM((GROUPS, D3 * GROUP, LANES), BF),
+            pltpu.VMEM((D1 * D2, LANES, LANES), BF),
+            pltpu.VMEM((D1 * D2, SLOTS, LANES), BF),
             pltpu.VMEM((D2, 4 * SLOTS, LANES), BF),
             pltpu.VMEM((D2, 4 * SLOTS, LANES), BF),
             pltpu.VMEM((2, D1, SLOTS, LANES), F32),
             pltpu.VMEM((2, SLOTS, SLOTS), BF),
-            pltpu.VMEM((8, D1 * GROUP, R), BF),
+            pltpu.VMEM((GROUPS, D1 * GROUP, R), BF),
         ],
         interpret=INTERPRET,
         name="terms",

time: 114 us -> 107 us (0.939)
  Pallas kernels: 41.6 us -> 34.3 us
    pallas_call x1, Pallas kernels: 22.6 us -> 15.4 us  [terms(): pl.pallas_call(terms_kernel, out_shape=(jax.ShapeDtypeStruct(half, F32),...]
  transfers between devices with their start and end apart: 10 -> 10, of which waited for: 5 -> 5; matrix products, arithmetic and copies ran while one was open for 1% -> 1% of each run, Pallas kernels for 13% -> 14%
where the time goes in v4:
time: 107 us; the launch traced here: 106 us
  blocking collectives  37.6 us (35%)
  Pallas kernels  34.3 us (32%)
  starting transfers between devices  14.4 us (13%)
  waiting for transfers between devices  13.5 us (13%)
  local copies, waits for them, and re-layouts  2.9 us (3%)
  other arithmetic  2.41 us (2%)
    all_to_all x1, blocking collectives, local(): mine = lax.all_to_all(packed, 'dp', split_axis=0, concat_axis=0, tiled=True)  37.6 us
    pallas_call x1, Pallas kernels, terms(): pl.pallas_call(terms_kernel, out_shape=(jax.ShapeDtypeStruct(half, F32),...  15.4 us
    pallas_call x1, Pallas kernels, mid_step(): pl.pallas_call(mid_kernel, grid=(R // R_BLOCK,), out_shape=tuple((jax.Sha...  8.86 us
    ppermute x1, waiting for transfers between devices, local(): far = lax.ppermute(near, 'rep', CHIP_SWAP)  8.07 us
    all_to_all x1, starting transfers between devices, local(): lax.all_to_all(chip_sum, 'dp', split_axis=0, concat_axis=0, tiled=True)  6.34 us
    pallas_call x1, Pallas kernels, mid_round(): pl.pallas_call(mid_copy_kernel, grid=(R // R_BLOCK,), out_shape=jax.Shape...  5.89 us
    unnamed x22, local copies, waits for them, and re-layouts  2.9 us
    ppermute x1, starting transfers between devices, local(): theirs = lax.ppermute(mine, 'rep', CORE_SWAP)  2.88 us
  transfers between devices with their start and end apart: 10, of which 5 were waited for; matrix products, arithmetic and copies ran while one was open for 1% of the time, Pallas kernels for 14%

profile of v4, /device:TPU:1, one launch (start us, length us, event | category | flops | bytes accessed | tf_op | source)
XLA Modules:
  0.0 105.9 jit_solution(2996277211887012125)
XLA Ops:
  0.7 2.4 %pack.1 = bf16[512,768]{1,0:T(8,128)(2,1)} custom-call(s32[1]{0:T(128)} %bitcast.side_ref, s32[1,256]{1,0:T(1,128)} %bitcast.49, s32[1,256]{1,0:T(1,128)} %bitcast.50, s32[1,256]{1,0:T(1,128)} %bitcast.51, s32[1,16]{1,0:T(1,128)} %bag_ref.1, bf16[16,128]{1,0:T(8,128)(2,1)} %cot_ref.1, f32[8,512]{1,0:T(8,128)} %refs_0_.1, f32[8,512]{1,0:T(8,128)} %refs_3_.1), custom_call_target="tpu_custom_call" | custom-call | tf_op jit(solution)/shard_map/pack/pallas_call | solution.py:105
  3.0 37.6 %all_to_all.23 = bf16[64,8,768]{2,1,0:T(8,128)(2,1)S(1)} all-to-all(bf16[64,8,768]{2,1,0:T(8,128)(2,1)} %bitcast.43), channel_id=1, replica_groups=mesh['rep'=4,'dp'=64] {'dp'}, dimensions={0} | all-to-all | bytes 1572864 | tf_op jit(solution)/shard_map/all_to_all | solution.py:384
  40.7 2.9 %collective-permute-start = (bf16[512,768]{1,0:T(8,128)(2,1)S(1)}, bf16[512,768]{1,0:T(8,128)(2,1)S(1)}, u32[]{:S(2)}, u32[]{:S(2)}) collective-permute-start(bf16[512,768]{1,0:T(8,128)(2,1)S(1)} %bitcast.44), channel_id=1, source_target_pairs={{0,64},{64,0},{128,192},{192,128},{1,65},{65,1},{129,193},{193,129... | collective-permute-start | bytes 2359304 | tf_op jit(solution)/shard_map/ppermute | solution.py:386
  43.5 5.9 %mid_round.1.mid_ref = bf16[4,8,128,128]{3,2,1,0:T(8,128)(2,1)} custom-call(f32[4096,128]{1,0:T(8,128)} %bitcast.41), custom_call_target="tpu_custom_call" | custom-call | tf_op jit(solution)/shard_map/mid_round/pallas_call | solution.py:265
  49.4 0.9 copy-done.3
  50.3 15.4 %terms.1 = (f32[2,8,128,128]{3,2,1,0:T(8,128)}, f32[2,8,128,128]{3,2,1,0:T(8,128)}, f32[512,512]{1,0:T(8,128)}, f32[512,512]{1,0:T(8,128)}) custom-call(s32[1]{0:T(128)} %bitcast.side_ref, bf16[512,768]{1,0:T(8,128)(2,1)} %bitcast.45, bf16[512,768]{1,0:T(8,128)(2,1)} %copy-done.3, bf16[4,8,128,128]{3,2,1,0:T(8,128)(2,1)} %mid_round.1.mid_ref), custom_call_target="tpu_custom_call" | custom-call | tf_op jit(solution)/shard_map/terms/pallas_call | solution.py:229
  65.9 0.3 collective-permute-start.2
  66.2 2.4 %collective-permute-done.1 = f32[2,8,128,128]{3,2,1,0:T(8,128)S(1)} collective-permute-done((f32[2,8,128,128]{3,2,1,0:T(8,128)}, f32[2,8,128,128]{3,2,1,0:T(8,128)S(1)}, u32[]{:S(2)}, u32[]{:S(2)}) %collective-permute-start.1) | collective-permute-done | bytes 1048608 | tf_op jit(solution)/shard_map/ppermute | solution.py:389
  68.6 1.3 %add_convert_fusion.1.near_ref = bf16[2,8,128,128]{3,2,1,0:T(8,128)(2,1)S(1)} fusion(f32[2,8,128,128]{3,2,1,0:T(8,128)} %get-tuple-element.28, f32[2,8,128,128]{3,2,1,0:T(8,128)S(1)} %collective-permute-done.1), kind=kLoop, calls=%fused_computation.2 | loop fusion | flops 524288 | bytes 2621440 | tf_op jit(solution)/shard_map/convert_element_type | solution.py:391
  70.1 1.0 add_convert_fusion
  71.0 0.4 collective-permute-start.3
  71.4 6.3 %all-to-all-start.1 = ((bf16[64,8,512]{2,1,0:T(8,128)(2,1)}), bf16[64,8,512]{2,1,0:T(8,128)(2,1)S(1)}, u32[]{:S(2)}, u32[]{:S(2)}) async-start(bf16[64,8,512]{2,1,0:T(8,128)(2,1)} %bitcast.9), calls=%async_computation.1 | async-start | bytes 1048576 | tf_op jit(solution)/shard_map/all_to_all | solution.py:394
  77.8 0.8 collective-permute-start.4
  78.6 8.1 %collective-permute-done.3.far_ref = bf16[2,8,128,128]{3,2,1,0:T(8,128)(2,1)S(1)} collective-permute-done((bf16[2,8,128,128]{3,2,1,0:T(8,128)(2,1)S(1)}, bf16[2,8,128,128]{3,2,1,0:T(8,128)(2,1)S(1)}, u32[]{:S(2)}, u32[]{:S(2)}) %collective-permute-start.3) | collective-permute-done | bytes 524320 | tf_op jit(solution)/shard_map/ppermute | solution.py:393
  86.7 1.5 %collective-permute-start.5 = (bf16[2,8,128,128]{3,2,1,0:T(8,128)(2,1)S(1)}, bf16[2,8,128,128]{3,2,1,0:T(8,128)(2,1)S(1)}, u32[]{:S(2)}, u32[]{:S(2)}) collective-permute-start(bf16[2,8,128,128]{3,2,1,0:T(8,128)(2,1)S(1)} %collective-permute-done.3.far_ref), channel_id=1, source_target_pairs={{0,64},{64,0},{128,192},{192,128},{1,65},{65,1},{129,193},{193,129... | collective-permute-start | bytes 1572872 | tf_op jit(solution)/shard_map/ppermute | solution.py:396
  88.2 1.5 %collective-permute-done.5.far_rest_ref = bf16[2,8,128,128]{3,2,1,0:T(8,128)(2,1)S(1)} collective-permute-done((bf16[2,8,128,128]{3,2,1,0:T(8,128)(2,1)S(1)}, bf16[2,8,128,128]{3,2,1,0:T(8,128)(2,1)S(1)}, u32[]{:S(2)}, u32[]{:S(2)}) %collective-permute-start.5) | collective-permute-done | bytes 524320 | tf_op jit(solution)/shard_map/ppermute | solution.py:396
  89.8 0.8 copy-done.6
  90.6 8.9 %mid_step.1 = (f32[4096,128]{1,0:T(8,128)}, f32[4096,128]{1,0:T(8,128)}, f32[4096,128]{1,0:T(8,128)}) custom-call(s32[1]{0:T(128)} %bitcast.side_ref, f32[4096,128]{1,0:T(8,128)} %bitcast.42, f32[4096,128]{1,0:T(8,128)} %bitcast.47, f32[4096,128]{1,0:T(8,128)} %bitcast.48, bf16[2,8,128,128]{3,2,1,0:T(8,128)(2,1)} %copy-done.1, ...), custom_call_target="tpu_custom_call" | custom-call | tf_op jit(solution)/shard_map/mid_step/pallas_call | solution.py:298
  99.5 0.4 collective-permute-start.8
  100.1 1.4 %collective-permute-start.6 = (f32[8,512]{1,0:T(8,128)S(1)}, f32[8,512]{1,0:T(8,128)S(1)}, u32[]{:S(2)}, u32[]{:S(2)}) collective-permute-start(f32[8,512]{1,0:T(8,128)S(1)} %convert_reduce_fusion.own_ref), channel_id=1, source_target_pairs={{0,128},{128,0},{64,192},{192,64},{1,129},{129,1},{65,193},{193,65... | collective-permute-start | bytes 49160 | tf_op jit(solution)/shard_map/ppermute | solution.py:407
  101.5 1.4 %collective-permute-done.8.both_ref = f32[8,512]{1,0:T(8,128)S(1)} collective-permute-done((f32[8,512]{1,0:T(8,128)S(1)}, f32[8,512]{1,0:T(8,128)S(1)}, u32[]{:S(2)}, u32[]{:S(2)}) %collective-permute-start.8) | collective-permute-done | bytes 16416 | tf_op jit(solution)/shard_map/ppermute | solution.py:407
  102.9 0.6 copy-done.8
  103.5 0.6 copy-done.10
  104.1 1.8 %outer.1 = (f32[8,512]{1,0:T(8,128)}, f32[8,512]{1,0:T(8,128)}, f32[8,512]{1,0:T(8,128)}, f32[8,512]{1,0:T(8,128)}, f32[8,512]{1,0:T(8,128)}, /*index=5*/f32[8,512]{1,0:T(8,128)}) custom-call(s32[1]{0:T(128)} %bitcast.side_ref, f32[8,512]{1,0:T(8,128)} %copy-done.7, f32[8,512]{1,0:T(8,128)} %copy-done.10, f32[8,512]{1,0:T(8,128)} %copy-done.9, ...), custom_call_target="tpu_custom_call" | custom-call | tf_op jit(solution)/shard_map/outer/pallas_call | solution.py:333
  (27 shorter events, 0.7 us)
Async XLA Ops:
  40.7 8.8 %copy-start = (bf16[64,8,768]{2,1,0:T(8,128)(2,1)}, bf16[64,8,768]{2,1,0:T(8,128)(2,1)S(1)}, u32[]{:S(2)}) copy-start(bf16[64,8,768]{2,1,0:T(8,128)(2,1)S(1)} %all_to_all.23) | copy-start | bytes 2359300
  40.7 8.8 %collective-permute-start = (bf16[512,768]{1,0:T(8,128)(2,1)S(1)}, bf16[512,768]{1,0:T(8,128)(2,1)S(1)}, u32[]{:S(2)}, u32[]{:S(2)}) collective-permute-start(bf16[512,768]{1,0:T(8,128)(2,1)S(1)} %bitcast.44), channel_id=1, source_target_pairs={{0,64},{64,0},{128,192},{192,128},{1,65},{65,1},{129,193},{193,129... | collective-permute-start | bytes 2359304 | tf_op jit(solution)/shard_map/ppermute | solution.py:386
  49.4 0.9 copy-start.3
  65.7 4.4 %copy-start.2 = (f32[512,512]{1,0:T(8,128)S(1)}, f32[512,512]{1,0:T(8,128)}, u32[]{:S(2)}) copy-start(f32[512,512]{1,0:T(8,128)} %get-tuple-element.30) | copy-start | bytes 3145732
  65.7 2.9 %collective-permute-start.1 = (f32[2,8,128,128]{3,2,1,0:T(8,128)}, f32[2,8,128,128]{3,2,1,0:T(8,128)S(1)}, u32[]{:S(2)}, u32[]{:S(2)}) collective-permute-start(f32[2,8,128,128]{3,2,1,0:T(8,128)} %get-tuple-element.29), channel_id=1, source_target_pairs={{0,64},{64,0},{128,192},{192,128},{1,65},{65,1},{129,193},{193,129... | collective-permute-start | bytes 3145736 | tf_op jit(solution)/shard_map/ppermute | solution.py:389
  65.9 4.2 %collective-permute-start.2 = (f32[512,512]{1,0:T(8,128)}, f32[512,512]{1,0:T(8,128)S(1)}, u32[]{:S(2)}, u32[]{:S(2)}) collective-permute-start(f32[512,512]{1,0:T(8,128)} %get-tuple-element.31), channel_id=1, source_target_pairs={{0,64},{64,0},{128,192},{192,128},{1,65},{65,1},{129,193},{193,129... | collective-permute-start | bytes 3145736 | tf_op jit(solution)/shard_map/ppermute | solution.py:390
  69.9 19.9 %copy-start.1 = (bf16[2,8,128,128]{3,2,1,0:T(8,128)(2,1)}, bf16[2,8,128,128]{3,2,1,0:T(8,128)(2,1)S(1)}, u32[]{:S(2)}) copy-start(bf16[2,8,128,128]{3,2,1,0:T(8,128)(2,1)S(1)} %add_convert_fusion.1.near_ref) | copy-start | bytes 1572868
  71.0 15.7 %collective-permute-start.3 = (bf16[2,8,128,128]{3,2,1,0:T(8,128)(2,1)S(1)}, bf16[2,8,128,128]{3,2,1,0:T(8,128)(2,1)S(1)}, u32[]{:S(2)}, u32[]{:S(2)}) collective-permute-start(bf16[2,8,128,128]{3,2,1,0:T(8,128)(2,1)S(1)} %add_convert_fusion.1.near_ref), channel_id=1, source_target_pairs={{0,128},{128,0},{64,192},{192,64},{1,129},{129,1},{65,193},{193,65... | collective-permute-start | bytes 1572872 | tf_op jit(solution)/shard_map/ppermute | solution.py:393
  71.4 28.0 %all-to-all-start.1 = ((bf16[64,8,512]{2,1,0:T(8,128)(2,1)}), bf16[64,8,512]{2,1,0:T(8,128)(2,1)S(1)}, u32[]{:S(2)}, u32[]{:S(2)}) async-start(bf16[64,8,512]{2,1,0:T(8,128)(2,1)} %bitcast.9), calls=%async_computation.1 | async-start | bytes 1048576 | tf_op jit(solution)/shard_map/all_to_all | solution.py:394
  77.8 10.5 %collective-permute-start.4 = (bf16[2,8,128,128]{3,2,1,0:T(8,128)(2,1)S(1)}, bf16[2,8,128,128]{3,2,1,0:T(8,128)(2,1)S(1)}, u32[]{:S(2)}, u32[]{:S(2)}) collective-permute-start(bf16[2,8,128,128]{3,2,1,0:T(8,128)(2,1)S(1)} %add_convert_fusion.1.near_ref), channel_id=1, source_target_pairs={{0,64},{64,0},{128,192},{192,128},{1,65},{65,1},{129,193},{193,129... | collective-permute-start | bytes 1572872 | tf_op jit(solution)/shard_map/ppermute | solution.py:395
  86.7 3.1 %copy-start.4 = (bf16[2,8,128,128]{3,2,1,0:T(8,128)(2,1)}, bf16[2,8,128,128]{3,2,1,0:T(8,128)(2,1)S(1)}, u32[]{:S(2)}) copy-start(bf16[2,8,128,128]{3,2,1,0:T(8,128)(2,1)S(1)} %collective-permute-done.3.far_ref) | copy-start | bytes 1572868
  86.7 3.1 %collective-permute-start.5 = (bf16[2,8,128,128]{3,2,1,0:T(8,128)(2,1)S(1)}, bf16[2,8,128,128]{3,2,1,0:T(8,128)(2,1)S(1)}, u32[]{:S(2)}, u32[]{:S(2)}) collective-permute-start(bf16[2,8,128,128]{3,2,1,0:T(8,128)(2,1)S(1)} %collective-permute-done.3.far_ref), channel_id=1, source_target_pairs={{0,64},{64,0},{128,192},{192,128},{1,65},{65,1},{129,193},{193,129... | collective-permute-start | bytes 1572872 | tf_op jit(solution)/shard_map/ppermute | solution.py:396
  88.2 1.5 %copy-start.5 = (bf16[2,8,128,128]{3,2,1,0:T(8,128)(2,1)}, bf16[2,8,128,128]{3,2,1,0:T(8,128)(2,1)S(1)}, u32[]{:S(2)}) copy-start(bf16[2,8,128,128]{3,2,1,0:T(8,128)(2,1)S(1)} %collective-permute-done.4.near_rest_ref) | copy-start | bytes 1572868
  89.8 0.8 copy-start.6
  99.5 3.3 %copy-start.7 = (f32[8,512]{1,0:T(8,128)}, f32[8,512]{1,0:T(8,128)S(1)}, u32[]{:S(2)}) copy-start(f32[8,512]{1,0:T(8,128)S(1)} %convert_reduce_fusion.own_ref) | copy-start | bytes 49156
  99.5 3.3 %collective-permute-start.8 = (f32[8,512]{1,0:T(8,128)S(1)}, f32[8,512]{1,0:T(8,128)S(1)}, u32[]{:S(2)}, u32[]{:S(2)}) collective-permute-start(f32[8,512]{1,0:T(8,128)S(1)} %convert_reduce_fusion.own_ref), channel_id=1, source_target_pairs={{0,192},{192,0},{64,128},{128,64},{1,193},{193,1},{65,129},{129,65... | collective-permute-start | bytes 49160 | tf_op jit(solution)/shard_map/ppermute | solution.py:407
  99.9 3.0 %collective-permute-start.7 = (f32[8,512]{1,0:T(8,128)S(1)}, f32[8,512]{1,0:T(8,128)S(1)}, u32[]{:S(2)}, u32[]{:S(2)}) collective-permute-start(f32[8,512]{1,0:T(8,128)S(1)} %convert_reduce_fusion.own_ref), channel_id=1, source_target_pairs={{0,64},{64,0},{128,192},{192,128},{1,65},{65,1},{129,193},{193,129... | collective-permute-start | bytes 49160 | tf_op jit(solution)/shard_map/ppermute | solution.py:407
  100.1 2.8 %collective-permute-start.6 = (f32[8,512]{1,0:T(8,128)S(1)}, f32[8,512]{1,0:T(8,128)S(1)}, u32[]{:S(2)}, u32[]{:S(2)}) collective-permute-start(f32[8,512]{1,0:T(8,128)S(1)} %convert_reduce_fusion.own_ref), channel_id=1, source_target_pairs={{0,128},{128,0},{64,192},{192,64},{1,129},{129,1},{65,193},{193,65... | collective-permute-start | bytes 49160 | tf_op jit(solution)/shard_map/ppermute | solution.py:407
  102.9 0.6 copy-start.8
  102.9 0.6 copy-start.9
  103.5 0.6 copy-start.10
